TPU v7x, 256 devices: a whole 4x4x8 slice. The times are simulated.
256 devices in a mesh: mp: 2 (over core), dev: 128 (over y, x, z).
Axes of the slice: x: 4, y: 4, z: 8, core: 2. Of those that a mesh axis runs over, the one named last changes fastest.
Arguments:
- spectrum: float32 [1024, 65536], P(None, ('mp', 'dev')), may hold values from 0.05 to 1
- water_mask: int32 [65536], P(('mp', 'dev')), may hold values 0 or 1
- courant: float32 [2, 1024], replicated, may hold values from 0.05 to 0.3
- stencil_sign: int32 [2, 1024], replicated, may hold values from 0 to 1
- quad_index: int32 [4, 1024, 2], replicated, may hold values from 0 to 1023
- quad_weight: float32 [4, 1024, 2], replicated, may hold values from 0.2 to 1
- nonlinear: float32 [1024], replicated, may hold values from 0.01 to 0.1
- stokes_table: bfloat16 [128, 1024], replicated, may hold values from -0.1875 to 0.1875
- point_index: int32 [4, 65536], P(None, ('mp', 'dev')), may hold values from 0 to 32767, as said below
- point_weight: float32 [4, 65536], P(None, ('mp', 'dev')), may hold values from 0.1 to 0.4
- ocean_index: int32 [4, 32768], P(None, ('mp', 'dev')), may hold values from 0 to 65535, as said below
- ocean_weight: float32 [4, 32768], P(None, ('mp', 'dev')), may hold values from 0.1 to 0.4
- currents: float32 [2, 64, 32768], P(None, None, ('mp', 'dev')), may hold values from -3 to 3
- coriolis: float32 [32768], P(('mp', 'dev')), may hold values from 0.2 to 0.6
- mixing: float32 [64], replicated, may hold values from 0.05 to 0.2
- surface_weights: float32 [64], replicated, may hold values from 0.005 to 0.05
Outputs:
- spectrum_out: float32 [1024, 65536], P(None, ('mp', 'dev'))
- currents_out: float32 [2, 64, 32768], P(None, None, ('mp', 'dev'))
Inputs may be any that keep to these rules, and one draw needn't show every extreme that they name: `point_index`: entry j of point p names an ocean cell in row p // 256 plus -1, 0 or 1 and column (p % 256) // 2 plus -1, 0 or 1, both wrapping. `ocean_index`: entry j of cell c names a wave point in row c // 128 plus -1, 0 or 1 and column 2 (c % 128) plus -2 to 3, both wrapping.
All inputs are finite; a program needn't handle non-finite values. No bound on the sum of `water_mask` on one device may be relied on, other than what follows from the above.
Results may differ from a plain program's by a relative error of at most 0.0003.
The roundings to bfloat16 on the way count: a program that leaves them out, or rounds other values in their place, can miss the bound.
Values sent between devices are 32-bit elements; how exact they have to be, the bound alone decides.
No kernel may reach another device: no remote copies, remote signals or barrier semaphores. Data moves between devices by JAX's collectives and lax.ppermute only.
A program may use at most 64 MiB of HBM per device.

v0:
```python
import functools

import jax
import jax.numpy as jnp
from jax import lax
from jax.experimental import pallas as pl
from jax.experimental.pallas import tpu as pltpu
from jax.sharding import PartitionSpec as P

K = 1024
L = 64
MX = 256
OX = 128
AXES = ("mp", "dev")
EXTRA = 72
LIMIT = 24 << 20
FAST = 576
F32 = jnp.float32
BF16 = jnp.bfloat16
VMEM = pl.BlockSpec(memory_space=pltpu.VMEM)
SMEM = pl.BlockSpec(memory_space=pltpu.SMEM)
HIGHEST = lax.Precision.HIGHEST


def dot_nt(a, b):
    return lax.dot_general(a, b, (((1,), (1,)), ((), ())), preferred_element_type=F32)


def dot_nn(a, b):
    return jnp.dot(a, b, preferred_element_type=F32)


def dot_exact(a, b):
    return jnp.dot(a, b, precision=HIGHEST, preferred_element_type=F32)


def split3(x):
    high = x.astype(BF16)
    rest = x - high.astype(F32)
    middle = rest.astype(BF16)
    low = (rest - middle.astype(F32)).astype(BF16)
    return high, middle, low


def one_hot_rows(select_ref, pos_ref, copies=1):
    place = lax.broadcasted_iota(jnp.int32, (K, 128), 0).astype(F32)
    for block in range(8):
        hit = place == pos_ref[block : block + 1, :]
        ones = jnp.where(hit, 1.0, 0.0).astype(BF16)
        for copy in range(copies):
            start = copy * K + block * 128
            select_ref[:, start : start + 128] = ones


def pack_kernel(
    count, sign, spectrum, currents, level, coriolis, ocean_index, ocean_weight,
    up, down, pos, surface, zonal, fits, select, parts,
):
    for block in range(8):
        pos[block : block + 1, :] = sign[1:2, block * 128 : (block + 1) * 128].astype(F32)
    ones = pos[...]
    upper = lax.broadcasted_iota(jnp.int32, (128, 128), 0) <= lax.broadcasted_iota(
        jnp.int32, (128, 128), 1
    )
    before = dot_nn(ones.astype(BF16), jnp.where(upper, 1.0, 0.0).astype(BF16))
    running = jnp.zeros((1, 1), F32)
    counts = []
    for block in range(8):
        counts.append(before[block : block + 1, :] + running)
        running = running + before[block : block + 1, 127:128]
    northward = jnp.sum(running)
    fits[0] = jnp.logical_and(northward <= count, K - northward <= count).astype(jnp.int32)
    lane = lax.broadcasted_iota(jnp.int32, (1, 128), 1).astype(F32)
    for block in range(8):
        index = lane + float(block * 128)
        first = counts[block] - 1.0
        second = running + index - counts[block]
        pos[block : block + 1, :] = jnp.where(ones[block : block + 1, :] > 0.5, first, second)
    one_hot_rows(select, pos, 3)
    high, middle, low = split3(spectrum[...])
    parts[0:K, :] = low
    parts[K : 2 * K, :] = middle
    parts[2 * K :, :] = high
    value = dot_nn(select[...], parts[...])
    up[0:count, :] = value[0:count, :]
    down[0:count, :] = value[K - count :, :]
    weights = jnp.broadcast_to(level[...], (8, L))
    flat_u = dot_exact(weights, currents[0])
    flat_v = dot_exact(weights, currents[1])
    surface[...] = flat_u
    surface[1:2, :] = flat_v[0:1, :]
    zonal[...] = currents[0]
    half = L // 2
    for message in (up, down):
        message[count : count + 1, 0:OX] = flat_u[0:1, :]
        message[count : count + 1, OX : 2 * OX] = flat_v[0:1, :]
        message[count + 1 : count + 5, 0:OX] = ocean_index[...].astype(F32)
        message[count + 1 : count + 5, OX : 2 * OX] = ocean_weight[...]
        message[count + 5 : count + 8, :] = jnp.zeros((3, MX), F32)
        message[count + 5 : count + 6, 0:OX] = coriolis[...]
        for flow in range(2):
            at = count + 8 + flow * half
            message[at : at + half, 0:OX] = currents[flow, 0:half, :]
            message[at : at + half, OX : 2 * OX] = currents[flow, half:, :]


def table_kernel(
    row, pos, sign, courant, nonlinear, quad_index, quad_weight, stokes_table, point_index,
    point_weight, mixing, level, quad, back, stokes_sorted, wide, cell_column, cell_side, cell_weight,
    mixing_wide, level_wide, select, rows, parts, columns,
):
    one_hot_rows(select, pos)
    sense = (2 * sign[...] - 1).astype(F32)
    speed = courant[...]
    rows[...] = jnp.zeros((32, K), F32)
    rows[0:2, :] = speed
    rows[2:4, :] = 0.5 * speed * sense
    rows[4:6, :] = sense
    rows[6:7, :] = nonlinear[...]
    for config in range(4):
        index = quad_index[config]
        weight = quad_weight[config]
        same = index[0:1] == index[1:2]
        first = jnp.where(same, weight[0:1] + weight[1:2], weight[0:1])
        second = jnp.where(same, 0.0, weight[1:2])
        rows[8 + 2 * config : 9 + 2 * config, :] = first.astype(BF16).astype(F32)
        rows[9 + 2 * config : 10 + 2 * config, :] = second.astype(BF16).astype(F32)
        rows[16 + 2 * config : 18 + 2 * config, :] = index.astype(F32)
    high, middle, low = split3(rows[...])
    parts[0:32, :] = high
    parts[32:64, :] = middle
    parts[64:96, :] = low
    component = lax.broadcasted_iota(jnp.int32, (16, K), 1)
    line = lax.broadcasted_iota(jnp.int32, (16, K), 0)
    digits = jnp.where(line == 0, component // 32, component % 32).astype(F32).astype(BF16)
    found = dot_nt(digits, select[...])
    order = found[0:1] * 32.0 + found[1:2]
    stokes_sorted[...] = dot_nt(stokes_table[...], select[...]).astype(BF16)

    got = dot_nt(select[...], parts[...])
    columns[...] = got[:, 0:32] + (got[:, 32:64] + got[:, 64:96])

    def block_rows(block, carry):
        at = pl.ds(pl.multiple_of(block * 64, 64), 64)
        column = columns[at, :]
        for item in range(7):
            wide[item, at, :] = jnp.broadcast_to(column[:, item : item + 1], (64, 128))
        original = (lax.broadcasted_iota(jnp.int32, (64, K), 0) + block * 64).astype(F32)
        back[at, :] = jnp.where(order == original, 1.0, 0.0).astype(BF16)
        for config in range(4):
            a = 8 + 2 * config
            b = 16 + 2 * config
            value = jnp.where(
                order == column[:, b : b + 1],
                column[:, a : a + 1],
                jnp.where(order == column[:, b + 1 : b + 2], column[:, a + 1 : a + 2], 0.0),
            )
            quad[config, at, :] = value.astype(BF16)
        return carry

    lax.fori_loop(0, K // 64, block_rows, 0)
    for config in range(4):
        for half in range(2):
            line = slice(2 * config + half, 2 * config + half + 1)
            cell = point_index[config : config + 1, half * 128 : (half + 1) * 128]
            cell_column[line, :] = cell % OX
            cell_side[line, :] = (cell // OX - row[0] + 257) % 256
            cell_weight[line, :] = point_weight[config : config + 1, half * 128 : (half + 1) * 128]
    diagonal = lax.broadcasted_iota(jnp.int32, (L, L), 0) == lax.broadcasted_iota(jnp.int32, (L, L), 1)
    for line, wide_column in ((mixing, mixing_wide), (level, level_wide)):
        column = jnp.sum(jnp.where(diagonal, line[...], 0.0), axis=1, keepdims=True)
        wide_column[...] = jnp.broadcast_to(column, (L, OX))


def cell_table(base, index, weight):
    point = (lax.broadcasted_iota(jnp.int32, (MX, OX), 0) + base).astype(F32)
    total = jnp.zeros((MX, OX), F32)
    for config in range(4):
        total = total + jnp.where(
            index[config : config + 1, :] == point, weight[config : config + 1, :], 0.0
        )
    return total


def update(count, own_up, own_down, from_below, from_above, flow, quad, wide, stokes_sorted, wet,
           advected, rounded, interp):
    bend_x = jnp.tanh(flow[0])
    bend_y = jnp.tanh(flow[1])
    skip = K - count
    size = 64

    def advect(start, own, shift, behind):
        def body(block, carry):
            at = pl.multiple_of(block * size + start, size)
            here = own[pl.ds(at - shift, size), :]
            west = pltpu.roll(here, 1, 1)
            east = pltpu.roll(here, MX - 1, 1)

            def both(item):
                half = wide[item, pl.ds(at, size), :]
                return jnp.concatenate([half, half], axis=1)

            behind_x = jnp.where(both(4) > 0.0, west, east)
            speed_x = both(0) + both(2) * bend_x
            speed_y = both(1) + both(3) * bend_y
            value = here - speed_x * (here - behind_x) - speed_y * (here - behind(at, both))
            advected[pl.ds(at, size), :] = value
            rounded[pl.ds(at, size), :] = value.astype(BF16)
            return carry

        return body

    def below(at, both):
        return from_below[pl.ds(at, size), :]

    def above(at, both):
        return from_above[pl.ds(at - skip, size), :]

    def either(at, both):
        return jnp.where(both(5) > 0.0, below(at, both), above(at, both))

    if skip:
        lax.fori_loop(0, skip // size, advect(0, own_up, 0, below), 0)
    lax.fori_loop(0, (count - skip) // size, advect(skip, own_up, 0, either), 0)
    if skip:
        lax.fori_loop(0, skip // size, advect(count, own_down, skip, above), 0)

    def member(config, carry):
        interp[config] = dot_nn(quad[config], rounded[...])
        return carry

    lax.fori_loop(0, 4, member, 0)

    def source(block, carry):
        at = pl.ds(pl.multiple_of(block * size, size), size)
        members = [interp[config, at, :] for config in range(4)]
        value = advected[at, :]
        pairs = members[0] * members[1] + members[2] * members[3]
        total = (members[0] + members[1]) + (members[2] + members[3])
        gain = wide[6, at, :]
        gain = jnp.concatenate([gain, gain], axis=1)
        result = wet * (value + gain * (value * (value * total - pairs)))
        advected[at, :] = result
        rounded[at, :] = result.astype(BF16)
        return carry

    lax.fori_loop(0, K // size, source, 0)
    return dot_nn(stokes_sorted[...], rounded[...])


def flow_of(sides, column, side, weight):
    index = column[...]
    where = side[...]
    flow = []
    for component in range(2):
        total = jnp.zeros((8, OX), F32)
        for item in range(3):
            line = jnp.broadcast_to(sides[item][:, component * OX : (component + 1) * OX], (8, OX))
            got = jnp.take_along_axis(line, index, axis=1, mode="promise_in_bounds")
            total = jnp.where(where == item, got, total)
        total = total * weight[...]
        halves = [
            (total[h : h + 1] + total[h + 2 : h + 3]) + (total[h + 4 : h + 5] + total[h + 6 : h + 7])
            for h in range(2)
        ]
        flow.append(jnp.concatenate(halves, axis=1))
    return flow


def drift_parts(stokes, cells, cells_low):
    high = stokes.astype(BF16)
    low = (stokes - high.astype(F32)).astype(BF16)
    both = dot_nn(jnp.concatenate([high, low], axis=0), cells[...])
    return both[0:128] + (both[128:] + dot_nn(high, cells_low[...]))


def tall(block):
    return jnp.concatenate([block[:, 0:OX], block[:, OX:]], axis=0)


def turn(v, u_below, u_above):
    return 0.5 * (pltpu.roll(v, OX - 1, 1) - pltpu.roll(v, 1, 1)) - 0.5 * (u_above - u_below)


def mix(profile, mixing):
    line = lax.broadcasted_iota(jnp.int32, (L, OX), 0)
    before = jnp.where(line == 0, profile, pltpu.roll(profile, 1, 0))
    after = jnp.where(line == L - 1, profile, pltpu.roll(profile, L - 1, 0))
    return mixing * (before - 2.0 * profile + after)


def ocean_step(u, v, u_below, u_above, drift, rotation, mixing):
    vorticity = turn(v, u_below, u_above)
    drift_x = drift[0:L, :]
    drift_y = drift[L:, :]
    new_u = u + 0.5 * (rotation * (v + drift_y) + vorticity * drift_y + mix(u, mixing))
    new_v = v + 0.5 * (-rotation * (u + drift_x) - vorticity * drift_x + mix(v, mixing))
    return new_u, new_v


def level_sum(weights, x):
    return jnp.sum(weights * x, axis=0, keepdims=True)


def first_kernel(
    count, row, own_up, own_down, from_below, from_above, below_two, above_two, surface, quad, wide,
    stokes_sorted, cell_column, cell_side, cell_weight, wet, ocean_index, ocean_weight, currents,
    coriolis, mixing, level,
    up, down, own_part, surface_part, far_up, far_down, cells, cells_low, advected, rounded, interp,
):
    base = row[0] * MX
    half = L // 2
    below_extra = from_below[count:, :]
    above_extra = from_above[count:, :]
    for side, index, weight in (
        (0, below_extra[1:5, 0:OX], below_extra[1:5, OX:]),
        (1, ocean_index[...].astype(F32), ocean_weight[...]),
        (2, above_extra[1:5, 0:OX], above_extra[1:5, OX:]),
    ):
        table = cell_table(base, index, weight)
        high = table.astype(BF16)
        cells[:, side * OX : (side + 1) * OX] = high
        cells_low[:, side * OX : (side + 1) * OX] = (table - high.astype(F32)).astype(BF16)
    own = jnp.concatenate([surface[0:1, :], surface[1:2, :]], axis=1)
    sides = (below_extra[0:1, :], own, above_extra[0:1, :])
    flow = flow_of(sides, cell_column, cell_side, cell_weight)
    wet_row = wet[...].astype(F32)
    stokes = update(count, own_up, own_down, from_below, from_above, flow, quad, wide, stokes_sorted,
                    wet_row, advected, rounded, interp)
    up[0:count, :] = advected[0:count, :]
    down[0:count, :] = advected[K - count :, :]
    part = drift_parts(stokes, cells, cells_low)
    u, v = currents[0], currents[1]
    u_below, v_below = tall(below_extra[8 : 8 + half]), tall(below_extra[8 + half : 8 + 2 * half])
    u_above, v_above = tall(above_extra[8 : 8 + half]), tall(above_extra[8 + half : 8 + 2 * half])
    weights = level[...]
    rotations = (below_extra[5:6, 0:OX], coriolis[...], above_extra[5:6, 0:OX])
    turns = (turn(v_below, below_two[...], u), turn(v, u_below, u_above), turn(v_above, u, above_two[...]))
    shares = []
    for side in range(3):
        factor = 0.5 * weights * (rotations[side] + turns[side])
        block = part[:, side * OX : (side + 1) * OX]
        shares.append((jnp.sum(factor * block[L:], axis=0, keepdims=True),
                       -jnp.sum(factor * block[0:L], axis=0, keepdims=True)))
    own_u = shares[1][0] + level_sum(weights, u + 0.5 * (coriolis[...] * v + mix(u, mixing[...])))
    own_v = shares[1][1] + level_sum(weights, v + 0.5 * (mix(v, mixing[...]) - coriolis[...] * u))
    own_part[...] = part[:, OX : 2 * OX]
    surface_part[...] = jnp.zeros((8, MX), F32)
    for side, message, far in ((0, down, far_down), (2, up, far_up)):
        block = part[:, side * OX : (side + 1) * OX]
        message[count : count + L, 0:OX] = block[0:L]
        message[count : count + L, OX:] = block[L:]
        message[count + L :, :] = jnp.zeros((8, MX), F32)
        message[count + L : count + L + 1, 0:OX] = own_u
        message[count + L : count + L + 1, OX:] = own_v
        message[count + L + 1 : count + L + 2, 0:OX] = shares[side][0]
        message[count + L + 1 : count + L + 2, OX:] = shares[side][1]
        far[...] = jnp.zeros((8, MX), F32)
        far[0:1, 0:OX] = shares[side][0]
        far[0:1, OX:] = shares[side][1]
        at = side // 2
        surface_part[at : at + 1, 0:OX] = shares[side][0]
        surface_part[at : at + 1, OX:] = shares[side][1]
    surface_part[2:3, 0:OX] = own_u
    surface_part[2:3, OX:] = own_v


def second_kernel(
    count, own_up, own_down, from_below, from_above, below_two, above_two, zonal_below, zonal_above,
    own_part, surface_part, quad, wide, stokes_sorted, cell_column, cell_side, cell_weight, wet, cells,
    cells_low, currents, coriolis, mixing,
    spectra, state, to_above, to_below, last_part, rounded, interp,
):
    half = L // 2
    below_extra = from_below[count:, :]
    above_extra = from_above[count:, :]
    own = surface_part[...]
    surf_below = below_extra[L : L + 1] + below_two[0:1, :] + own[0:1]
    surf_own = own[2:3] + below_extra[L + 1 : L + 2] + above_extra[L + 1 : L + 2]
    surf_above = above_extra[L : L + 1] + above_two[0:1, :] + own[1:2]
    flow = flow_of((surf_below, surf_own, surf_above), cell_column, cell_side, cell_weight)
    drift = own_part[...] + tall(below_extra[0:L]) + tall(above_extra[0:L])
    new_u, new_v = ocean_step(
        currents[0], currents[1], tall(zonal_below[count + 8 : count + 8 + half, :]),
        tall(zonal_above[count + 8 : count + 8 + half, :]), drift, coriolis[...], mixing[...]
    )
    state[0] = new_u
    state[1] = new_v
    wet_row = wet[...].astype(F32)
    stokes = update(count, own_up, own_down, from_below, from_above, flow, quad, wide, stokes_sorted,
                    wet_row, spectra, rounded, interp)
    part = drift_parts(stokes, cells, cells_low)
    to_below[0:128, :] = part[:, 0:OX]
    last_part[...] = part[:, OX : 2 * OX]
    to_above[0:128, :] = part[:, 2 * OX :]
    to_below[128:, :] = new_u
    to_above[128:, :] = new_u


def restore_kernel(spectra, back, out, parts):
    high, middle, low = split3(spectra[...])
    parts[0] = low
    parts[1] = middle
    parts[2] = high
    out[...] = jnp.zeros((K, MX), F32)

    def add(item, carry):
        out[...] += dot_nn(back[...], parts[item])
        return carry

    lax.fori_loop(0, 3, add, 0)


def last_ocean(state, from_below, from_above, own_part, coriolis, mixing, out):
    drift = own_part[...] + from_below[0:128, :] + from_above[0:128, :]
    new_u, new_v = ocean_step(
        state[0], state[1], from_below[128:, :], from_above[128:, :], drift, coriolis[...], mixing[...]
    )
    out[0] = new_u
    out[1] = new_v


def shape(*dims, dtype=F32):
    return jax.ShapeDtypeStruct(dims, dtype)


def call(body, outs, scratch=(), scalars=0, inputs=0, flops=0, data=0, name=None, out_specs=None):
    return pl.pallas_call(
        body,
        out_shape=outs,
        in_specs=[SMEM] * scalars + [VMEM] * (inputs - scalars),
        out_specs=out_specs or jax.tree.map(lambda _: VMEM, outs),
        scratch_shapes=scratch,
        cost_estimate=pl.CostEstimate(flops=flops, bytes_accessed=data, transcendentals=0),
        compiler_params=pltpu.CompilerParams(vmem_limit_bytes=LIMIT),
        name=name,
    )


def exchange(to_above, to_below, distance=1):
    total = lax.axis_size("mp") * lax.axis_size("dev")
    up = [(i, (i + distance) % total) for i in range(total)]
    return (
        lax.ppermute(to_above, AXES, up),
        lax.ppermute(to_below, AXES, [(b, a) for a, b in up]),
    )


def pack(count, stencil_sign, spectrum, currents, level, coriolis, ocean_index, ocean_weight):
    message = shape(count + EXTRA, MX)
    return call(
        functools.partial(pack_kernel, count),
        (message, message, shape(8, 128), shape(8, 128), shape(L, OX), shape(1, dtype=jnp.int32)),
        (pltpu.VMEM((K, 3 * K), BF16), pltpu.VMEM((3 * K, MX), BF16)),
        inputs=7, flops=2 * K * K * 3 * MX, data=1 << 20, name="pack",
        out_specs=(VMEM, VMEM, VMEM, VMEM, VMEM, SMEM),
    )(stencil_sign, spectrum, currents, level, coriolis, ocean_index, ocean_weight)


def steps(
    count, packed, row, wet, courant, stencil_sign, quad_index, quad_weight, nonlinear, stokes_table,
    point_index, point_weight, ocean_index, ocean_weight, currents, coriolis, mixing, level,
):
    up, down, pos, surface, zonal = packed
    part = shape(128, OX)
    message = shape(count + EXTRA, MX)
    far = shape(8, MX)
    table = shape(MX, 3 * OX, dtype=BF16)
    work = (pltpu.VMEM((K, MX), BF16), pltpu.VMEM((4, K, MX), F32))
    below, above = exchange(up, down)
    whole = jnp.int32
    quad, back, stokes_sorted, wide, cell_column, cell_side, cell_weight, mixing, level = call(
        table_kernel,
        (
            shape(4, K, K, dtype=BF16), shape(K, K, dtype=BF16), shape(128, K, dtype=BF16),
            shape(7, K, 128), shape(8, OX, dtype=whole), shape(8, OX, dtype=whole), shape(8, OX),
            shape(L, OX), shape(L, OX),
        ),
        (pltpu.VMEM((K, K), BF16), pltpu.VMEM((32, K), F32), pltpu.VMEM((96, K), BF16),
         pltpu.VMEM((K, 32), F32)),
        scalars=1, inputs=12, flops=4 << 30, data=12 << 20, name="tables",
    )(row, pos, stencil_sign, courant, nonlinear, quad_index, quad_weight, stokes_table, point_index,
      point_weight, mixing, level)
    below_two, above_two = exchange(zonal, zonal, 2)
    next_up, next_down, own_part, surface_part, far_up, far_down, cells, cells_low = call(
        functools.partial(first_kernel, count),
        (message, message, part, far, far, far, table, table),
        (pltpu.VMEM((K, MX), F32),) + work,
        scalars=1, inputs=21, flops=3 << 30, data=12 << 20, name="first",
    )(row, up, down, below, above, below_two, above_two, surface, quad, wide, stokes_sorted,
      cell_column, cell_side, cell_weight, wet, ocean_index, ocean_weight, currents, coriolis, mixing,
      level)
    next_below, next_above = exchange(next_up, next_down)
    far_below, far_above = exchange(far_up, far_down, 2)
    end = shape(128 + L, OX)
    spectra, state, to_above, to_below, last_part = call(
        functools.partial(second_kernel, count),
        (shape(K, MX), shape(2, L, OX), end, end, part),
        work, inputs=22, flops=3 << 30, data=12 << 20, name="second",
    )(next_up, next_down, next_below, next_above, far_below, far_above, below, above, own_part,
      surface_part, quad, wide, stokes_sorted, cell_column, cell_side, cell_weight, wet, cells,
      cells_low, currents, coriolis, mixing)
    end_below, end_above = exchange(to_above, to_below)
    out = call(
        restore_kernel, shape(K, MX), (pltpu.VMEM((3, K, MX), BF16),), inputs=2, flops=2 * K * K * 3 * MX, data=4 << 20, name="restore",
    )(spectra, back)
    final = call(
        last_ocean, shape(2, L, OX), inputs=6, flops=1 << 20, data=1 << 18, name="ocean",
    )(state, end_below, end_above, last_part, coriolis, mixing)
    return out, final


def local(
    spectrum, water_mask, courant, stencil_sign, quad_index, quad_weight, nonlinear, stokes_table,
    point_index, point_weight, ocean_index, ocean_weight, currents, coriolis, mixing, surface_weights,
):
    row = (lax.axis_index("mp") * lax.axis_size("dev") + lax.axis_index("dev")).reshape(1)
    rotation = coriolis.reshape(1, OX)
    level = surface_weights.reshape(1, L)
    to_pack = (stencil_sign, spectrum, currents, level, rotation, ocean_index, ocean_weight)
    *packed, fits = pack(FAST, *to_pack)
    rest = (
        row.astype(jnp.int32),
        water_mask.reshape(1, MX),
        courant,
        stencil_sign,
        quad_index.transpose(0, 2, 1),
        quad_weight.transpose(0, 2, 1),
        nonlinear.reshape(1, K),
        stokes_table,
        point_index,
        point_weight,
        ocean_index,
        ocean_weight,
        currents,
        rotation,
        mixing.reshape(1, L),
        level,
    )

    def balanced(packed, to_pack, rest):
        return steps(FAST, packed, *rest)

    def general(packed, to_pack, rest):
        return steps(K, pack(K, *to_pack)[:-1], *rest)

    return lax.cond(fits[0] == 1, balanced, general, tuple(packed), to_pack, rest)


def solution(mesh):
    whole = P(AXES)
    last = P(None, AXES)
    return jax.shard_map(
        local,
        mesh=mesh,
        in_specs=(
            last, whole, P(), P(), P(), P(), P(), P(), last, last, last, last,
            P(None, None, AXES), whole, P(), P(),
        ),
        out_specs=(last, P(None, None, AXES)),
        check_vma=False,
    )
```

profile of v0, /device:TPU:1, one launch (start us, length us, event | category | flops | bytes accessed | tf_op | source)
XLA Modules:
  0.0 81.2 jit_solution(17343819893282372741)
XLA Ops:
  0.8 4.0 %pack.3 = (f32[648,256]{1,0:T(8,128)S(1)}, f32[648,256]{1,0:T(8,128)S(1)}, f32[8,128]{1,0:T(8,128)S(1)}, f32[8,128]{1,0:T(8,128)S(1)}, f32[64,128]{1,0:T(8,128)S(1)}, /*index=5*/s32[1]{0:T(128)}) custom-call(s32[2,1024]{1,0:T(2,128)} %sign.1, f32[1024,256]{1,0:T(8,128)} %spectrum.1, f32[2,64,128]{2,1,0:T(8,128)} %currents.1, f32[1,64]{1,0:T(1,128)} %bitcast.20, ...), custom_call_target="tpu_custom_call" | custom-call | flops 1610612736 | bytes 1048576 | tf_op jit(solution)/shard_map/pack/pallas_call | solution.py:451
  5.6 75.6 %conditional.1 = (f32[1024,256]{1,0:T(8,128)}, f32[2,64,128]{2,1,0:T(8,128)}) conditional(s32[]{:T(128)} %bitcast.2, (s32[2,1024]{1,0:T(2,128)S(1)}, f32[1024,256]{1,0:T(8,128)S(1)}, f32[2,64,128]{2,1,0:T(8,128)S(1)}, f32[1,64]{1,0:T(1,128)S(1)}, f32[1,128]{1,0:T(1,128)S(1)}, /*index=5*/s32[4,128]{1,0:T(4,128)S(1)}, f32[4,128]{1,0:T(4,128)S(1)}, ...), branch_computations={%region_0.0_spmd, %region_1.0_spmd} | conditional | flops 13959692288 | bytes 62325152 | solution.py:547
  5.9 2.5 %collective-permute-start.10 = (f32[648,256]{1,0:T(8,128)S(1)}, f32[648,256]{1,0:T(8,128)S(1)}, u32[]{:S(2)}, u32[]{:S(2)}) collective-permute-start(f32[648,256]{1,0:T(8,128)S(1)} %get-tuple-element.121.own_up), channel_id=1, source_target_pairs={{0,1},{1,2},{2,3},{3,4},{4,5},{5,6},{6,7},{7,8},{8,9},{9,10},{10,1... | collective-permute-start | bytes 1990664 | tf_op jit(solution)/shard_map/cond/branch_1_fun/ppermute | solution.py:444
  8.4 9.2 %collective-permute-start.11 = (f32[648,256]{1,0:T(8,128)S(1)}, f32[648,256]{1,0:T(8,128)S(1)}, u32[]{:S(2)}, u32[]{:S(2)}) collective-permute-start(f32[648,256]{1,0:T(8,128)S(1)} %get-tuple-element.122.own_down), channel_id=1, source_target_pairs={{1,0},{2,1},{3,2},{4,3},{5,4},{6,5},{7,6},{8,7},{9,8},{10,9},{11,1... | collective-permute-start | bytes 1990664 | tf_op jit(solution)/shard_map/cond/branch_1_fun/ppermute | solution.py:445
  17.6 2.4 %collective-permute-start.13 = (f32[64,128]{1,0:T(8,128)S(1)}, f32[64,128]{1,0:T(8,128)S(1)}, u32[]{:S(2)}, u32[]{:S(2)}) collective-permute-start(f32[64,128]{1,0:T(8,128)S(1)} %get-tuple-element.123), channel_id=1, source_target_pairs={{2,0},{3,1},{4,2},{5,3},{6,4},{7,5},{8,6},{9,7},{10,8},{11,9},{12,... | collective-permute-start | bytes 98312 | tf_op jit(solution)/shard_map/cond/branch_1_fun/ppermute | solution.py:445
  20.0 0.0 collective-permute-start.12
  20.0 7.5 %tables.3 = (bf16[4,1024,1024]{2,1,0:T(8,128)(2,1)S(1)}, bf16[1024,1024]{1,0:T(8,128)(2,1)S(1)}, bf16[128,1024]{1,0:T(8,128)(2,1)S(1)}, f32[7,1024,128]{2,1,0:T(...) custom-call(s32[1]{0:T(128)} %get-tuple-element.120.row, ...), custom_call_target="tpu_custom_call" | custom-call | flops 4294967296 | bytes 12582912 | tf_op jit(solution)/shard_map/cond/branch_1_fun/tables/pallas_call | solution.py:472
  27.5 6.2 %collective-permute-done.13.above_two = f32[64,128]{1,0:T(8,128)S(1)} collective-permute-done((f32[64,128]{1,0:T(8,128)S(1)}, f32[64,128]{1,0:T(8,128)S(1)}, u32[]{:S(2)}, u32[]{:S(2)}) %collective-permute-start.13) | collective-permute-done | bytes 32800 | tf_op jit(solution)/shard_map/cond/branch_1_fun/ppermute | solution.py:445
  33.8 0.6 collective-permute-done.12.below_two
  34.4 0.0 collective-permute-done.10.from_below.zonal_below
  34.4 0.0 collective-permute-done.11.from_above.zonal_above
  34.4 6.1 %first.3 = (f32[648,256]{1,0:T(8,128)S(1)}, f32[648,256]{1,0:T(8,128)S(1)}, f32[128,128]{1,0:T(8,128)S(1)}, f32[8,256]{1,0:T(8,128)S(1)}, f32[8,256]{1,0:T(8,128...) custom-call(s32[1]{0:T(128)} %get-tuple-element.120.row, ...), custom_call_target="tpu_custom_call" | custom-call | flops 3221225472 | bytes 12582912 | tf_op jit(solution)/shard_map/cond/branch_1_fun/first/pallas_call | solution.py:485
  40.5 0.1 collective-permute-start.14
  40.6 7.2 %collective-permute-start.15 = (f32[648,256]{1,0:T(8,128)S(1)}, f32[648,256]{1,0:T(8,128)S(1)}, u32[]{:S(2)}, u32[]{:S(2)}) collective-permute-start(f32[648,256]{1,0:T(8,128)S(1)} %get-tuple-element.150.own_down), channel_id=1, source_target_pairs={{1,0},{2,1},{3,2},{4,3},{5,4},{6,5},{7,6},{8,7},{9,8},{10,9},{11,1... | collective-permute-start | bytes 1990664 | tf_op jit(solution)/shard_map/cond/branch_1_fun/ppermute | solution.py:445
  47.7 0.0 collective-permute-start.16
  47.8 8.1 %collective-permute-start.17 = (f32[8,256]{1,0:T(8,128)S(1)}, f32[8,256]{1,0:T(8,128)S(1)}, u32[]{:S(2)}, u32[]{:S(2)}) collective-permute-start(f32[8,256]{1,0:T(8,128)S(1)} %get-tuple-element.152), channel_id=1, source_target_pairs={{2,0},{3,1},{4,2},{5,3},{6,4},{7,5},{8,6},{9,7},{10,8},{11,9},{12,... | collective-permute-start | bytes 24584 | tf_op jit(solution)/shard_map/cond/branch_1_fun/ppermute | solution.py:445
  55.8 8.0 %collective-permute-done.16.below_two = f32[8,256]{1,0:T(8,128)S(1)} collective-permute-done((f32[8,256]{1,0:T(8,128)S(1)}, f32[8,256]{1,0:T(8,128)S(1)}, u32[]{:S(2)}, u32[]{:S(2)}) %collective-permute-start.16) | collective-permute-done | bytes 8224 | tf_op jit(solution)/shard_map/cond/branch_1_fun/ppermute | solution.py:444
  63.8 0.0 collective-permute-done.17.above_two
  63.8 0.0 collective-permute-done.14.from_below
  63.8 6.0 %second.3 = (f32[1024,256]{1,0:T(8,128)S(1)}, f32[2,64,128]{2,1,0:T(8,128)S(1)}, f32[192,128]{1,0:T(8,128)S(1)}, f32[192,128]{1,0:T(8,128)S(1)}, f32[128,128]{1,0:T(8,128)S(1)}) custom-call(f32[648,256]{1,0:T(8,128)S(1)} %get-tuple-element.149.own_up, f32[648,256]{1,0:T(8,128)S(1)} %get-tuple-element.150.own_down, ...), custom_call_target="tpu_custom_call" | custom-call | flops 3221225472 | bytes 12582912 | tf_op jit(solution)/shard_map/cond/branch_1_fun/second/pallas_call | solution.py:496
  69.8 0.1 collective-permute-start.18
  69.9 7.2 %collective-permute-start.19 = (f32[192,128]{1,0:T(8,128)S(1)}, f32[192,128]{1,0:T(8,128)S(1)}, u32[]{:S(2)}, u32[]{:S(2)}) collective-permute-start(f32[192,128]{1,0:T(8,128)S(1)} %get-tuple-element.161), channel_id=1, source_target_pairs={{1,0},{2,1},{3,2},{4,3},{5,4},{6,5},{7,6},{8,7},{9,8},{10,9},{11,1... | collective-permute-start | bytes 294920 | tf_op jit(solution)/shard_map/cond/branch_1_fun/ppermute | solution.py:445
  77.0 3.5 %restore.3 = f32[1024,256]{1,0:T(8,128)} custom-call(f32[1024,256]{1,0:T(8,128)S(1)} %get-tuple-element.157.spectra, bf16[1024,1024]{1,0:T(8,128)(2,1)S(1)} %get-tuple-element.158.back), custom_call_target="tpu_custom_call" | custom-call | flops 1610612736 | bytes 4194304 | tf_op jit(solution)/shard_map/cond/branch_1_fun/restore/pallas_call | solution.py:504
  80.5 0.7 ocean.3
  (35 shorter events, 0.1 us)
Async XLA Ops:
  0.6 4.8 %copy-start = (f32[2,64,128]{2,1,0:T(8,128)S(1)}, f32[2,64,128]{2,1,0:T(8,128)}, u32[]{:S(2)}) copy-start(f32[2,64,128]{2,1,0:T(8,128)} %currents.1) | copy-start | bytes 196612
  0.7 4.8 %copy-start.1 = (f32[128]{0:T(128)S(1)}, f32[128]{0:T(128)}, u32[]{:S(2)}) copy-start(f32[128]{0:T(128)} %param.31) | copy-start | bytes 1540
  0.7 4.8 %copy-start.2 = (s32[256]{0:T(256)S(1)}, s32[256]{0:T(256)}, u32[]{:S(2)}) copy-start(s32[256]{0:T(256)} %param.19) | copy-start | bytes 3076
  0.7 4.8 %copy-start.3 = (s32[4,128]{1,0:T(4,128)S(1)}, s32[4,128]{1,0:T(4,128)}, u32[]{:S(2)}) copy-start(s32[4,128]{1,0:T(4,128)} %ocean_index.1) | copy-start | bytes 6148
  0.7 4.8 %copy-start.4 = (f32[4,128]{1,0:T(4,128)S(1)}, f32[4,128]{1,0:T(4,128)}, u32[]{:S(2)}) copy-start(f32[4,128]{1,0:T(4,128)} %ocean_weight.1) | copy-start | bytes 6148
  0.7 4.8 %copy-start.5 = (f32[1024,256]{1,0:T(8,128)S(1)}, f32[1024,256]{1,0:T(8,128)}, u32[]{:S(2)}) copy-start(f32[1024,256]{1,0:T(8,128)} %spectrum.1) | copy-start | bytes 3145732
  0.7 4.8 %copy-start.6 = (bf16[128,1024]{1,0:T(8,128)(2,1)S(1)}, bf16[128,1024]{1,0:T(8,128)(2,1)}, u32[]{:S(2)}) copy-start(bf16[128,1024]{1,0:T(8,128)(2,1)} %param.25) | copy-start | bytes 786436
  0.7 4.8 %copy-start.7 = (s32[4,1024,2]{1,2,0:T(2,128)S(1)}, s32[4,1024,2]{1,2,0:T(2,128)}, u32[]{:S(2)}) copy-start(s32[4,1024,2]{1,2,0:T(2,128)} %param.22) | copy-start | bytes 98308
  0.7 4.8 %copy-start.8 = (f32[4,1024,2]{1,2,0:T(2,128)S(1)}, f32[4,1024,2]{1,2,0:T(2,128)}, u32[]{:S(2)}) copy-start(f32[4,1024,2]{1,2,0:T(2,128)} %param.23) | copy-start | bytes 98308
  0.7 4.8 %copy-start.9 = (s32[2,1024]{1,0:T(2,128)S(1)}, s32[2,1024]{1,0:T(2,128)}, u32[]{:S(2)}) copy-start(s32[2,1024]{1,0:T(2,128)} %sign.1) | copy-start | bytes 24580
  0.7 4.8 %copy-start.10 = (f32[2,1024]{1,0:T(2,128)S(1)}, f32[2,1024]{1,0:T(2,128)}, u32[]{:S(2)}) copy-start(f32[2,1024]{1,0:T(2,128)} %param.20) | copy-start | bytes 24580
  0.8 4.8 %copy-start.11 = (f32[1024]{0:T(1024)S(1)}, f32[1024]{0:T(1024)}, u32[]{:S(2)}) copy-start(f32[1024]{0:T(1024)} %param.24) | copy-start | bytes 12292
  0.8 4.8 %copy-start.12 = (s32[4,256]{1,0:T(4,128)S(1)}, s32[4,256]{1,0:T(4,128)}, u32[]{:S(2)}) copy-start(s32[4,256]{1,0:T(4,128)} %param.26) | copy-start | bytes 12292
  0.8 4.8 %copy-start.13 = (f32[4,256]{1,0:T(4,128)S(1)}, f32[4,256]{1,0:T(4,128)}, u32[]{:S(2)}) copy-start(f32[4,256]{1,0:T(4,128)} %param.27) | copy-start | bytes 12292
  5.9 28.5 %collective-permute-start.10 = (f32[648,256]{1,0:T(8,128)S(1)}, f32[648,256]{1,0:T(8,128)S(1)}, u32[]{:S(2)}, u32[]{:S(2)}) collective-permute-start(f32[648,256]{1,0:T(8,128)S(1)} %get-tuple-element.121.own_up), channel_id=1, source_target_pairs={{0,1},{1,2},{2,3},{3,4},{4,5},{5,6},{6,7},{7,8},{8,9},{9,10},{10,1... | collective-permute-start | bytes 1990664 | tf_op jit(solution)/shard_map/cond/branch_1_fun/ppermute | solution.py:444
  8.4 26.0 %collective-permute-start.11 = (f32[648,256]{1,0:T(8,128)S(1)}, f32[648,256]{1,0:T(8,128)S(1)}, u32[]{:S(2)}, u32[]{:S(2)}) collective-permute-start(f32[648,256]{1,0:T(8,128)S(1)} %get-tuple-element.122.own_down), channel_id=1, source_target_pairs={{1,0},{2,1},{3,2},{4,3},{5,4},{6,5},{7,6},{8,7},{9,8},{10,9},{11,1... | collective-permute-start | bytes 1990664 | tf_op jit(solution)/shard_map/cond/branch_1_fun/ppermute | solution.py:445
  17.6 16.1 %collective-permute-start.13 = (f32[64,128]{1,0:T(8,128)S(1)}, f32[64,128]{1,0:T(8,128)S(1)}, u32[]{:S(2)}, u32[]{:S(2)}) collective-permute-start(f32[64,128]{1,0:T(8,128)S(1)} %get-tuple-element.123), channel_id=1, source_target_pairs={{2,0},{3,1},{4,2},{5,3},{6,4},{7,5},{8,6},{9,7},{10,8},{11,9},{12,... | collective-permute-start | bytes 98312 | tf_op jit(solution)/shard_map/cond/branch_1_fun/ppermute | solution.py:445
  20.0 14.4 %collective-permute-start.12 = (f32[64,128]{1,0:T(8,128)S(1)}, f32[64,128]{1,0:T(8,128)S(1)}, u32[]{:S(2)}, u32[]{:S(2)}) collective-permute-start(f32[64,128]{1,0:T(8,128)S(1)} %get-tuple-element.123), channel_id=1, source_target_pairs={{0,2},{1,3},{2,4},{3,5},{4,6},{5,7},{6,8},{7,9},{8,10},{9,11},{10,... | collective-permute-start | bytes 98312 | tf_op jit(solution)/shard_map/cond/branch_1_fun/ppermute | solution.py:444
  40.5 23.3 %collective-permute-start.14 = (f32[648,256]{1,0:T(8,128)S(1)}, f32[648,256]{1,0:T(8,128)S(1)}, u32[]{:S(2)}, u32[]{:S(2)}) collective-permute-start(f32[648,256]{1,0:T(8,128)S(1)} %get-tuple-element.149.own_up), channel_id=1, source_target_pairs={{0,1},{1,2},{2,3},{3,4},{4,5},{5,6},{6,7},{7,8},{8,9},{9,10},{10,1... | collective-permute-start | bytes 1990664 | tf_op jit(solution)/shard_map/cond/branch_1_fun/ppermute | solution.py:444
  40.6 23.2 %collective-permute-start.15 = (f32[648,256]{1,0:T(8,128)S(1)}, f32[648,256]{1,0:T(8,128)S(1)}, u32[]{:S(2)}, u32[]{:S(2)}) collective-permute-start(f32[648,256]{1,0:T(8,128)S(1)} %get-tuple-element.150.own_down), channel_id=1, source_target_pairs={{1,0},{2,1},{3,2},{4,3},{5,4},{6,5},{7,6},{8,7},{9,8},{10,9},{11,1... | collective-permute-start | bytes 1990664 | tf_op jit(solution)/shard_map/cond/branch_1_fun/ppermute | solution.py:445
  47.7 16.1 %collective-permute-start.16 = (f32[8,256]{1,0:T(8,128)S(1)}, f32[8,256]{1,0:T(8,128)S(1)}, u32[]{:S(2)}, u32[]{:S(2)}) collective-permute-start(f32[8,256]{1,0:T(8,128)S(1)} %get-tuple-element.151), channel_id=1, source_target_pairs={{0,2},{1,3},{2,4},{3,5},{4,6},{5,7},{6,8},{7,9},{8,10},{9,11},{10,... | collective-permute-start | bytes 24584 | tf_op jit(solution)/shard_map/cond/branch_1_fun/ppermute | solution.py:444
  47.8 16.1 %collective-permute-start.17 = (f32[8,256]{1,0:T(8,128)S(1)}, f32[8,256]{1,0:T(8,128)S(1)}, u32[]{:S(2)}, u32[]{:S(2)}) collective-permute-start(f32[8,256]{1,0:T(8,128)S(1)} %get-tuple-element.152), channel_id=1, source_target_pairs={{2,0},{3,1},{4,2},{5,3},{6,4},{7,5},{8,6},{9,7},{10,8},{11,9},{12,... | collective-permute-start | bytes 24584 | tf_op jit(solution)/shard_map/cond/branch_1_fun/ppermute | solution.py:445
  69.8 10.7 %collective-permute-start.18 = (f32[192,128]{1,0:T(8,128)S(1)}, f32[192,128]{1,0:T(8,128)S(1)}, u32[]{:S(2)}, u32[]{:S(2)}) collective-permute-start(f32[192,128]{1,0:T(8,128)S(1)} %get-tuple-element.160), channel_id=1, source_target_pairs={{0,1},{1,2},{2,3},{3,4},{4,5},{5,6},{6,7},{7,8},{8,9},{9,10},{10,1... | collective-permute-start | bytes 294920 | tf_op jit(solution)/shard_map/cond/branch_1_fun/ppermute | solution.py:444
  69.9 10.6 %collective-permute-start.19 = (f32[192,128]{1,0:T(8,128)S(1)}, f32[192,128]{1,0:T(8,128)S(1)}, u32[]{:S(2)}, u32[]{:S(2)}) collective-permute-start(f32[192,128]{1,0:T(8,128)S(1)} %get-tuple-element.161), channel_id=1, source_target_pairs={{1,0},{2,1},{3,2},{4,3},{5,4},{6,5},{7,6},{8,7},{9,8},{10,9},{11,1... | collective-permute-start | bytes 294920 | tf_op jit(solution)/shard_map/cond/branch_1_fun/ppermute | solution.py:445
  (2 other events, 9.6 us)
where the time goes:
time: 81.4 us; the launch traced here: 81.2 us
  starting transfers between devices  36.7 us (45%)
  Pallas kernels  27.7 us (34%)
  waiting for transfers between devices  14.9 us (18%)
  between operations  1.55 us (2%)
    ppermute x5, starting transfers between devices, exchange(): lax.ppermute(to_below, AXES, [(b, a) for a, b in up])  34 us
    ppermute x5, waiting for transfers between devices, exchange(): lax.ppermute(to_above, AXES, up)  8.64 us
    pallas_call x1, Pallas kernels, steps(): call(table_kernel, (shape(4, K, K, dtype=BF16), shape(K, K, dtype=BF16),...  7.51 us
    ppermute x5, waiting for transfers between devices, exchange(): lax.ppermute(to_below, AXES, [(b, a) for a, b in up])  6.23 us
    pallas_call x1, Pallas kernels, steps(): call(functools.partial(first_kernel, count), (message, message, part, far...  6.08 us
    pallas_call x1, Pallas kernels, steps(): call(functools.partial(second_kernel, count), (shape(K, MX), shape(2, L,...  5.95 us
    pallas_call x1, Pallas kernels, pack(): call(functools.partial(pack_kernel, count), (message, message, shape(8, 1...  4 us
    pallas_call x1, Pallas kernels, steps(): call(restore_kernel, shape(K, MX), (pltpu.VMEM((3, K, MX), BF16),), input...  3.46 us
  transfers between devices with their start and end apart: 10, of which 3 were waited for; matrix products, arithmetic and copies ran while one was open for 0% of the time, Pallas kernels for 14%

commit v1 on v0

--- a/solution.py
+++ b/solution.py
@@ -14,7 +14,7 @@
 AXES = ("mp", "dev")
 EXTRA = 72
 LIMIT = 24 << 20
-FAST = 576
+FAST = 560
 F32 = jnp.float32
 BF16 = jnp.bfloat16
 VMEM = pl.BlockSpec(memory_space=pltpu.VMEM)
@@ -34,11 +34,14 @@
     return jnp.dot(a, b, precision=HIGHEST, preferred_element_type=F32)
 
 
+def split2(x):
+    high = x.astype(BF16)
+    return high, (x - high.astype(F32)).astype(BF16)
+
+
 def split3(x):
-    high = x.astype(BF16)
-    rest = x - high.astype(F32)
-    middle = rest.astype(BF16)
-    low = (rest - middle.astype(F32)).astype(BF16)
+    high, middle = split2(x)
+    low = (x - high.astype(F32) - middle.astype(F32)).astype(BF16)
     return high, middle, low
 
 
@@ -76,11 +79,10 @@
         first = counts[block] - 1.0
         second = running + index - counts[block]
         pos[block : block + 1, :] = jnp.where(ones[block : block + 1, :] > 0.5, first, second)
-    one_hot_rows(select, pos, 3)
-    high, middle, low = split3(spectrum[...])
+    one_hot_rows(select, pos, 2)
+    high, low = split2(spectrum[...])
     parts[0:K, :] = low
-    parts[K : 2 * K, :] = middle
-    parts[2 * K :, :] = high
+    parts[K:, :] = high
     value = dot_nn(select[...], parts[...])
     up[0:count, :] = value[0:count, :]
     down[0:count, :] = value[K - count :, :]
@@ -182,48 +184,65 @@
     return total
 
 
-def update(count, own_up, own_down, from_below, from_above, flow, quad, wide, stokes_sorted, wet,
+def blocks(start, stop, body):
+    for at in range(start, stop, 64):
+        body(at, min(64, stop - at))
+
+
+def slope_kernel(count, own_up, own_down, wide, slope):
+    def along(own, shift):
+        def body(at, size):
+            here = own[pl.ds(at - shift, size), :]
+            sense = wide[4, pl.ds(at, size), :]
+            sense = jnp.concatenate([sense, sense], axis=1)
+            behind = jnp.where(sense > 0.0, pltpu.roll(here, 1, 1), pltpu.roll(here, MX - 1, 1))
+            slope[pl.ds(at, size), :] = here - behind
+
+        return body
+
+    blocks(0, count, along(own_up, 0))
+    blocks(count, K, along(own_down, K - count))
+
+
+def update(count, own_up, own_down, from_below, from_above, flow, slope, quad, wide, stokes_sorted, wet,
            advected, rounded, interp):
     bend_x = jnp.tanh(flow[0])
     bend_y = jnp.tanh(flow[1])
     skip = K - count
-    size = 64
-
-    def advect(start, own, shift, behind):
-        def body(block, carry):
-            at = pl.multiple_of(block * size + start, size)
+
+    def advect(own, shift, behind):
+        def body(at, size):
             here = own[pl.ds(at - shift, size), :]
-            west = pltpu.roll(here, 1, 1)
-            east = pltpu.roll(here, MX - 1, 1)
-
-            def both(item):
-                half = wide[item, pl.ds(at, size), :]
-                return jnp.concatenate([half, half], axis=1)
-
-            behind_x = jnp.where(both(4) > 0.0, west, east)
-            speed_x = both(0) + both(2) * bend_x
-            speed_y = both(1) + both(3) * bend_y
-            value = here - speed_x * (here - behind_x) - speed_y * (here - behind(at, both))
-            advected[pl.ds(at, size), :] = value
-            rounded[pl.ds(at, size), :] = value.astype(BF16)
-            return carry
+            rows = pl.ds(at, size)
+            base_x, base_y, bend_of_x, bend_of_y = [wide[item, rows, :] for item in range(4)]
+            step_x = slope[rows, :]
+            step_y = here - behind(at, size)
+            for half in range(2):
+                lanes = slice(half * 128, (half + 1) * 128)
+                speed_x = base_x + bend_of_x * bend_x[:, lanes]
+                speed_y = base_y + bend_of_y * bend_y[:, lanes]
+                value = here[:, lanes] - speed_x * step_x[:, lanes] - speed_y * step_y[:, lanes]
+                advected[rows, lanes] = value
+                rounded[rows, lanes] = value.astype(BF16)
 
         return body
 
-    def below(at, both):
+    def below(at, size):
         return from_below[pl.ds(at, size), :]
 
-    def above(at, both):
+    def above(at, size):
         return from_above[pl.ds(at - skip, size), :]
 
-    def either(at, both):
-        return jnp.where(both(5) > 0.0, below(at, both), above(at, both))
+    def either(at, size):
+        sense = wide[5, pl.ds(at, size), :]
+        sense = jnp.concatenate([sense, sense], axis=1)
+        return jnp.where(sense > 0.0, below(at, size), above(at, size))
 
     if skip:
-        lax.fori_loop(0, skip // size, advect(0, own_up, 0, below), 0)
-    lax.fori_loop(0, (count - skip) // size, advect(skip, own_up, 0, either), 0)
+        blocks(0, skip, advect(own_up, 0, below))
+    blocks(skip, count, advect(own_up, 0, either))
     if skip:
-        lax.fori_loop(0, skip // size, advect(count, own_down, skip, above), 0)
+        blocks(count, K, advect(own_down, skip, above))
 
     def member(config, carry):
         interp[config] = dot_nn(quad[config], rounded[...])
@@ -231,8 +250,8 @@
 
     lax.fori_loop(0, 4, member, 0)
 
-    def source(block, carry):
-        at = pl.ds(pl.multiple_of(block * size, size), size)
+    def source(at, size):
+        at = pl.ds(at, size)
         members = [interp[config, at, :] for config in range(4)]
         value = advected[at, :]
         pairs = members[0] * members[1] + members[2] * members[3]
@@ -242,9 +261,8 @@
         result = wet * (value + gain * (value * (value * total - pairs)))
         advected[at, :] = result
         rounded[at, :] = result.astype(BF16)
-        return carry
-
-    lax.fori_loop(0, K // size, source, 0)
+
+    blocks(0, K, source)
     return dot_nn(stokes_sorted[...], rounded[...])
 
 
@@ -303,7 +321,7 @@
 
 
 def first_kernel(
-    count, row, own_up, own_down, from_below, from_above, below_two, above_two, surface, quad, wide,
+    count, row, own_up, own_down, from_below, from_above, below_two, above_two, surface, slope, quad, wide,
     stokes_sorted, cell_column, cell_side, cell_weight, wet, ocean_index, ocean_weight, currents,
     coriolis, mixing, level,
     up, down, own_part, surface_part, far_up, far_down, cells, cells_low, advected, rounded, interp,
@@ -325,8 +343,8 @@
     sides = (below_extra[0:1, :], own, above_extra[0:1, :])
     flow = flow_of(sides, cell_column, cell_side, cell_weight)
     wet_row = wet[...].astype(F32)
-    stokes = update(count, own_up, own_down, from_below, from_above, flow, quad, wide, stokes_sorted,
-                    wet_row, advected, rounded, interp)
+    stokes = update(count, own_up, own_down, from_below, from_above, flow, slope, quad, wide,
+                    stokes_sorted, wet_row, advected, rounded, interp)
     up[0:count, :] = advected[0:count, :]
     down[0:count, :] = advected[K - count :, :]
     part = drift_parts(stokes, cells, cells_low)
@@ -367,7 +385,7 @@
 
 def second_kernel(
     count, own_up, own_down, from_below, from_above, below_two, above_two, zonal_below, zonal_above,
-    own_part, surface_part, quad, wide, stokes_sorted, cell_column, cell_side, cell_weight, wet, cells,
+    own_part, surface_part, slope, quad, wide, stokes_sorted, cell_column, cell_side, cell_weight, wet, cells,
     cells_low, currents, coriolis, mixing,
     spectra, state, to_above, to_below, last_part, rounded, interp,
 ):
@@ -387,8 +405,8 @@
     state[0] = new_u
     state[1] = new_v
     wet_row = wet[...].astype(F32)
-    stokes = update(count, own_up, own_down, from_below, from_above, flow, quad, wide, stokes_sorted,
-                    wet_row, spectra, rounded, interp)
+    stokes = update(count, own_up, own_down, from_below, from_above, flow, slope, quad, wide,
+                    stokes_sorted, wet_row, spectra, rounded, interp)
     part = drift_parts(stokes, cells, cells_low)
     to_below[0:128, :] = part[:, 0:OX]
     last_part[...] = part[:, OX : 2 * OX]
@@ -398,17 +416,11 @@
 
 
 def restore_kernel(spectra, back, out, parts):
-    high, middle, low = split3(spectra[...])
-    parts[0] = low
-    parts[1] = middle
-    parts[2] = high
-    out[...] = jnp.zeros((K, MX), F32)
-
-    def add(item, carry):
-        out[...] += dot_nn(back[...], parts[item])
-        return carry
-
-    lax.fori_loop(0, 3, add, 0)
+    high, low = split2(spectra[...])
+    parts[:, 0:MX] = high
+    parts[:, MX:] = low
+    both = dot_nn(back[...], parts[...])
+    out[...] = both[:, 0:MX] + both[:, MX:]
 
 
 def last_ocean(state, from_below, from_above, own_part, coriolis, mixing, out):
@@ -447,29 +459,27 @@
 
 
 def pack(count, stencil_sign, spectrum, currents, level, coriolis, ocean_index, ocean_weight):
-    message = shape(count + EXTRA, MX)
+    message = pltpu.VMEM((count + EXTRA, MX), F32)
     return call(
         functools.partial(pack_kernel, count),
         (message, message, shape(8, 128), shape(8, 128), shape(L, OX), shape(1, dtype=jnp.int32)),
-        (pltpu.VMEM((K, 3 * K), BF16), pltpu.VMEM((3 * K, MX), BF16)),
+        (pltpu.VMEM((K, 2 * K), BF16), pltpu.VMEM((2 * K, MX), BF16)),
         inputs=7, flops=2 * K * K * 3 * MX, data=1 << 20, name="pack",
         out_specs=(VMEM, VMEM, VMEM, VMEM, VMEM, SMEM),
     )(stencil_sign, spectrum, currents, level, coriolis, ocean_index, ocean_weight)
 
 
-def steps(
-    count, packed, row, wet, courant, stencil_sign, quad_index, quad_weight, nonlinear, stokes_table,
-    point_index, point_weight, ocean_index, ocean_weight, currents, coriolis, mixing, level,
-):
-    up, down, pos, surface, zonal = packed
-    part = shape(128, OX)
-    message = shape(count + EXTRA, MX)
-    far = shape(8, MX)
-    table = shape(MX, 3 * OX, dtype=BF16)
-    work = (pltpu.VMEM((K, MX), BF16), pltpu.VMEM((4, K, MX), F32))
-    below, above = exchange(up, down)
+def slopes(count, up, down, wide):
+    return call(
+        functools.partial(slope_kernel, count), shape(K, MX), inputs=3, flops=1 << 30, data=4 << 20,
+        name="slopes",
+    )(up, down, wide)
+
+
+def tables(row, pos, stencil_sign, courant, nonlinear, quad_index, quad_weight, stokes_table, point_index,
+           point_weight, mixing, level):
     whole = jnp.int32
-    quad, back, stokes_sorted, wide, cell_column, cell_side, cell_weight, mixing, level = call(
+    return call(
         table_kernel,
         (
             shape(4, K, K, dtype=BF16), shape(K, K, dtype=BF16), shape(128, K, dtype=BF16),
@@ -481,28 +491,41 @@
         scalars=1, inputs=12, flops=4 << 30, data=12 << 20, name="tables",
     )(row, pos, stencil_sign, courant, nonlinear, quad_index, quad_weight, stokes_table, point_index,
       point_weight, mixing, level)
-    below_two, above_two = exchange(zonal, zonal, 2)
+
+
+def steps(
+    count, up, down, below, above, slope, below_two, above_two, surface, made, row, wet, ocean_index,
+    ocean_weight, currents, coriolis,
+):
+    quad, back, stokes_sorted, wide, cell_column, cell_side, cell_weight, mixing, level = made
+    part = shape(128, OX)
+    message = shape(count + EXTRA, MX)
+    far = shape(8, MX)
+    table = shape(MX, 3 * OX, dtype=BF16)
+    work = (pltpu.VMEM((K, MX), BF16), pltpu.VMEM((4, K, MX), F32))
     next_up, next_down, own_part, surface_part, far_up, far_down, cells, cells_low = call(
         functools.partial(first_kernel, count),
         (message, message, part, far, far, far, table, table),
         (pltpu.VMEM((K, MX), F32),) + work,
-        scalars=1, inputs=21, flops=3 << 30, data=12 << 20, name="first",
-    )(row, up, down, below, above, below_two, above_two, surface, quad, wide, stokes_sorted,
+        scalars=1, inputs=22, flops=3 << 30, data=12 << 20, name="first",
+    )(row, up, down, below, above, below_two, above_two, surface, slope, quad, wide, stokes_sorted,
       cell_column, cell_side, cell_weight, wet, ocean_index, ocean_weight, currents, coriolis, mixing,
       level)
     next_below, next_above = exchange(next_up, next_down)
     far_below, far_above = exchange(far_up, far_down, 2)
+    slope = slopes(count, next_up, next_down, wide)
     end = shape(128 + L, OX)
     spectra, state, to_above, to_below, last_part = call(
         functools.partial(second_kernel, count),
         (shape(K, MX), shape(2, L, OX), end, end, part),
-        work, inputs=22, flops=3 << 30, data=12 << 20, name="second",
+        work, inputs=23, flops=3 << 30, data=12 << 20, name="second",
     )(next_up, next_down, next_below, next_above, far_below, far_above, below, above, own_part,
-      surface_part, quad, wide, stokes_sorted, cell_column, cell_side, cell_weight, wet, cells,
+      surface_part, slope, quad, wide, stokes_sorted, cell_column, cell_side, cell_weight, wet, cells,
       cells_low, currents, coriolis, mixing)
     end_below, end_above = exchange(to_above, to_below)
     out = call(
-        restore_kernel, shape(K, MX), (pltpu.VMEM((3, K, MX), BF16),), inputs=2, flops=2 * K * K * 3 * MX, data=4 << 20, name="restore",
+        restore_kernel, shape(K, MX), (pltpu.VMEM((K, 2 * MX), BF16),), inputs=2, flops=2 * K * K * 2 * MX,
+        data=4 << 20, name="restore",
     )(spectra, back)
     final = call(
         last_ocean, shape(2, L, OX), inputs=6, flops=1 << 20, data=1 << 18, name="ocean",
@@ -515,36 +538,35 @@
     point_index, point_weight, ocean_index, ocean_weight, currents, coriolis, mixing, surface_weights,
 ):
     row = (lax.axis_index("mp") * lax.axis_size("dev") + lax.axis_index("dev")).reshape(1)
+    row = row.astype(jnp.int32)
     rotation = coriolis.reshape(1, OX)
     level = surface_weights.reshape(1, L)
     to_pack = (stencil_sign, spectrum, currents, level, rotation, ocean_index, ocean_weight)
-    *packed, fits = pack(FAST, *to_pack)
+    up, down, pos, surface, zonal, fits = pack(FAST, *to_pack)
+    below, above = exchange(up, down)
+    below = pltpu.with_memory_space_constraint(below, pltpu.VMEM)
+    above = pltpu.with_memory_space_constraint(above, pltpu.VMEM)
+    below_two, above_two = exchange(zonal, zonal, 2)
+    made = tables(
+        row, pos, stencil_sign, courant, nonlinear.reshape(1, K), quad_index.transpose(0, 2, 1),
+        quad_weight.transpose(0, 2, 1), stokes_table, point_index, point_weight, mixing.reshape(1, L),
+        level,
+    )
+    slope = slopes(FAST, up, down, made[3])
     rest = (
-        row.astype(jnp.int32),
-        water_mask.reshape(1, MX),
-        courant,
-        stencil_sign,
-        quad_index.transpose(0, 2, 1),
-        quad_weight.transpose(0, 2, 1),
-        nonlinear.reshape(1, K),
-        stokes_table,
-        point_index,
-        point_weight,
-        ocean_index,
-        ocean_weight,
-        currents,
-        rotation,
-        mixing.reshape(1, L),
-        level,
-    )
-
-    def balanced(packed, to_pack, rest):
-        return steps(FAST, packed, *rest)
-
-    def general(packed, to_pack, rest):
-        return steps(K, pack(K, *to_pack)[:-1], *rest)
-
-    return lax.cond(fits[0] == 1, balanced, general, tuple(packed), to_pack, rest)
+        below_two, above_two, surface, made, row, water_mask.reshape(1, MX), ocean_index, ocean_weight,
+        currents, rotation,
+    )
+
+    def balanced(sent, to_pack, rest):
+        return steps(FAST, *sent, *rest)
+
+    def general(sent, to_pack, rest):
+        up, down = pack(K, *to_pack)[:2]
+        below, above = exchange(up, down)
+        return steps(K, up, down, below, above, slopes(K, up, down, rest[3][3]), *rest)
+
+    return lax.cond(fits[0] == 1, balanced, general, (up, down, below, above, slope), to_pack, rest)
 
 
 def solution(mesh):

time: 81.4 us -> 75.2 us (0.924)
  Pallas kernels: 27.7 us -> 23.8 us
  waiting for transfers between devices: 14.9 us -> 12.7 us
    ppermute x5, waiting for transfers between devices: 6.23 us -> 4.43 us  [exchange(): lax.ppermute(to_below, AXES, [(b, a) for a, b in up])]
    pallas_call x1, Pallas kernels: 5.95 us -> 4.45 us  [steps(): call(functools.partial(second_kernel, count), (shape(K, MX), shape(2, L,...]
    pallas_call x1, Pallas kernels: 6.08 us -> 4.65 us  [steps(): call(functools.partial(first_kernel, count), (message, message, part, far...]
    pallas_call x1, Pallas kernels: 4 us -> 2.98 us  [pack(): call(functools.partial(pack_kernel, count), (message, message, shape(8, 1...]
    pallas_call x2 -> x4, Pallas kernels: 11 us -> 11 us  [the longest x1 7.52 us: tables(): call(table_kernel, (shape(4, K, K, dtype=BF16), shape(K, K, dtype=BF16),...]
  transfers between devices with their start and end apart: 10 -> 10, of which waited for: 3 -> 4; matrix products, arithmetic and copies ran while one was open for 0% -> 0% of each run, Pallas kernels for 14% -> 15%
where the time goes in v1:
time: 75.2 us; the launch traced here: 75.1 us
  starting transfers between devices  36.8 us (49%)
  Pallas kernels  23.8 us (32%)
  waiting for transfers between devices  12.7 us (17%)
  between operations  1.53 us (2%)
    ppermute x5, starting transfers between devices, exchange(): lax.ppermute(to_below, AXES, [(b, a) for a, b in up])  34 us
    ppermute x5, waiting for transfers between devices, exchange(): lax.ppermute(to_above, AXES, up)  8.27 us
    pallas_call x1, Pallas kernels, tables(): call(table_kernel, (shape(4, K, K, dtype=BF16), shape(K, K, dtype=BF16),...  7.52 us
    pallas_call x1, Pallas kernels, steps(): call(functools.partial(first_kernel, count), (message, message, part, far...  4.65 us
    pallas_call x1, Pallas kernels, steps(): call(functools.partial(second_kernel, count), (shape(K, MX), shape(2, L,...  4.45 us
    ppermute x5, waiting for transfers between devices, exchange(): lax.ppermute(to_below, AXES, [(b, a) for a, b in up])  4.43 us
    pallas_call x1, Pallas kernels, pack(): call(functools.partial(pack_kernel, count), (message, message, shape(8, 1...  2.98 us
    ppermute x5, starting transfers between devices, exchange(): lax.ppermute(to_above, AXES, up)  2.74 us
  transfers between devices with their start and end apart: 10, of which 4 were waited for; matrix products, arithmetic and copies ran while one was open for 0% of the time, Pallas kernels for 15%

profile of v1, /device:TPU:1, one launch (start us, length us, event | category | flops | bytes accessed | tf_op | source)
XLA Modules:
  0.0 75.1 jit_solution(506303486098598198)
XLA Ops:
  0.7 3.0 %pack.3 = (f32[632,256]{1,0:T(8,128)S(1)}, f32[632,256]{1,0:T(8,128)S(1)}, f32[8,128]{1,0:T(8,128)S(1)}, f32[8,128]{1,0:T(8,128)S(1)}, f32[64,128]{1,0:T(8,128)S(1)}, /*index=5*/s32[1]{0:T(128)}) custom-call(s32[2,1024]{1,0:T(2,128)} %sign.3, f32[1024,256]{1,0:T(8,128)} %spectrum.1, f32[2,64,128]{2,1,0:T(8,128)} %currents.1, f32[1,64]{1,0:T(1,128)} %bitcast.18, ...), custom_call_target="tpu_custom_call" | custom-call | flops 1610612736 | bytes 1048576 | tf_op jit(solution)/shard_map/pack/pallas_call | solution.py:463
  3.7 2.5 %collective-permute-start.16 = (f32[632,256]{1,0:T(8,128)S(1)}, f32[632,256]{1,0:T(8,128)S(1)}, u32[]{:S(2)}, u32[]{:S(2)}) collective-permute-start(f32[632,256]{1,0:T(8,128)S(1)} %get-tuple-element.190.own_up), channel_id=1, source_target_pairs={{0,1},{1,2},{2,3},{3,4},{4,5},{5,6},{6,7},{7,8},{8,9},{9,10},{10,1... | collective-permute-start | bytes 1941512 | tf_op jit(solution)/shard_map/ppermute | solution.py:456
  6.3 9.2 %collective-permute-start.17 = (f32[632,256]{1,0:T(8,128)S(1)}, f32[632,256]{1,0:T(8,128)S(1)}, u32[]{:S(2)}, u32[]{:S(2)}) collective-permute-start(f32[632,256]{1,0:T(8,128)S(1)} %get-tuple-element.191.own_down), channel_id=1, source_target_pairs={{1,0},{2,1},{3,2},{4,3},{5,4},{6,5},{7,6},{8,7},{9,8},{10,9},{11,1... | collective-permute-start | bytes 1941512 | tf_op jit(solution)/shard_map/ppermute | solution.py:457
  15.5 2.4 %collective-permute-start.15 = (f32[64,128]{1,0:T(8,128)S(1)}, f32[64,128]{1,0:T(8,128)S(1)}, u32[]{:S(2)}, u32[]{:S(2)}) collective-permute-start(f32[64,128]{1,0:T(8,128)S(1)} %get-tuple-element.180), channel_id=1, source_target_pairs={{2,0},{3,1},{4,2},{5,3},{6,4},{7,5},{8,6},{9,7},{10,8},{11,9},{12,... | collective-permute-start | bytes 98312 | tf_op jit(solution)/shard_map/ppermute | solution.py:457
  17.9 0.0 collective-permute-start.14
  18.0 7.5 %tables.1 = (bf16[4,1024,1024]{2,1,0:T(8,128)(2,1)S(1)}, bf16[1024,1024]{1,0:T(8,128)(2,1)S(1)}, bf16[128,1024]{1,0:T(8,128)(2,1)S(1)}, f32[7,1024,128]{2,1,0:T(...) custom-call(s32[1]{0:T(128)} %bitcast.3.row, ...), custom_call_target="tpu_custom_call" | custom-call | flops 4294967296 | bytes 12582912 | tf_op jit(solution)/shard_map/tables/pallas_call | solution.py:482
  25.5 0.0 copy-start.8
  25.5 0.0 copy-start.11
  25.6 0.6 slopes.7
  26.9 4.4 %collective-permute-done.15 = f32[64,128]{1,0:T(8,128)S(1)} collective-permute-done((f32[64,128]{1,0:T(8,128)S(1)}, f32[64,128]{1,0:T(8,128)S(1)}, u32[]{:S(2)}, u32[]{:S(2)}) %collective-permute-start.15) | collective-permute-done | bytes 32800 | tf_op jit(solution)/shard_map/ppermute | solution.py:457
  31.3 0.6 collective-permute-done.14
  32.0 43.1 %conditional.1 = (f32[1024,256]{1,0:T(8,128)}, f32[2,64,128]{2,1,0:T(8,128)}) conditional(s32[]{:T(128)} %bitcast.2, (s32[2,1024]{1,0:T(2,128)S(1)}, f32[1024,256]{1,0:T(8,128)S(1)}, f32[2,64,128]{2,1,0:T(8,128)S(1)}, f32[1,64]{1,0:T(1,128)S(1)}, f32[1,128]{1,0:T(1,128)S(1)}, /*index=5*/s32[4,128]{1,0:T(4,128)S(1)}, f32[4,128]{1,0:T(4,128)S(1)}, ...), branch_computations={%region_0.0_spmd, %region_1.0_spmd} | conditional | flops 11275337728 | bytes 57868624 | solution.py:569
  32.2 4.6 %first.3 = (f32[632,256]{1,0:T(8,128)S(1)}, f32[632,256]{1,0:T(8,128)S(1)}, f32[128,128]{1,0:T(8,128)S(1)}, f32[8,256]{1,0:T(8,128)S(1)}, f32[8,256]{1,0:T(8,128...) custom-call(s32[1]{0:T(128)} %get-tuple-element.124.row, ...), custom_call_target="tpu_custom_call" | custom-call | flops 3221225472 | bytes 12582912 | tf_op jit(solution)/shard_map/cond/branch_1_fun/first/pallas_call | solution.py:506
  36.9 0.1 collective-permute-start.8
  37.0 7.2 %collective-permute-start.9 = (f32[632,256]{1,0:T(8,128)S(1)}, f32[632,256]{1,0:T(8,128)S(1)}, u32[]{:S(2)}, u32[]{:S(2)}) collective-permute-start(f32[632,256]{1,0:T(8,128)S(1)} %get-tuple-element.147.own_down), channel_id=1, source_target_pairs={{1,0},{2,1},{3,2},{4,3},{5,4},{6,5},{7,6},{8,7},{9,8},{10,9},{11,1... | collective-permute-start | bytes 1941512 | tf_op jit(solution)/shard_map/cond/branch_1_fun/ppermute | solution.py:457
  44.1 8.1 %collective-permute-start.11 = (f32[8,256]{1,0:T(8,128)S(1)}, f32[8,256]{1,0:T(8,128)S(1)}, u32[]{:S(2)}, u32[]{:S(2)}) collective-permute-start(f32[8,256]{1,0:T(8,128)S(1)} %get-tuple-element.149), channel_id=1, source_target_pairs={{2,0},{3,1},{4,2},{5,3},{6,4},{7,5},{8,6},{9,7},{10,8},{11,9},{12,... | collective-permute-start | bytes 24584 | tf_op jit(solution)/shard_map/cond/branch_1_fun/ppermute | solution.py:457
  52.2 0.6 slopes.6.slope
  52.8 7.0 %collective-permute-done.10.below_two = f32[8,256]{1,0:T(8,128)S(1)} collective-permute-done((f32[8,256]{1,0:T(8,128)S(1)}, f32[8,256]{1,0:T(8,128)S(1)}, u32[]{:S(2)}, u32[]{:S(2)}) %collective-permute-start.10) | collective-permute-done | bytes 8224 | tf_op jit(solution)/shard_map/cond/branch_1_fun/ppermute | solution.py:456
  59.8 4.4 %second.3 = (f32[1024,256]{1,0:T(8,128)S(1)}, f32[2,64,128]{2,1,0:T(8,128)S(1)}, f32[192,128]{1,0:T(8,128)S(1)}, f32[192,128]{1,0:T(8,128)S(1)}, f32[128,128]{1,0:T(8,128)S(1)}) custom-call(f32[632,256]{1,0:T(8,128)S(1)} %get-tuple-element.146.own_up, f32[632,256]{1,0:T(8,128)S(1)} %get-tuple-element.147.own_down, ...), custom_call_target="tpu_custom_call" | custom-call | flops 3221225472 | bytes 12582912 | tf_op jit(solution)/shard_map/cond/branch_1_fun/second/pallas_call | solution.py:518
  64.3 0.1 collective-permute-start.12
  64.4 7.2 %collective-permute-start.13 = (f32[192,128]{1,0:T(8,128)S(1)}, f32[192,128]{1,0:T(8,128)S(1)}, u32[]{:S(2)}, u32[]{:S(2)}) collective-permute-start(f32[192,128]{1,0:T(8,128)S(1)} %get-tuple-element.158), channel_id=1, source_target_pairs={{1,0},{2,1},{3,2},{4,3},{5,4},{6,5},{7,6},{8,7},{9,8},{10,9},{11,1... | collective-permute-start | bytes 294920 | tf_op jit(solution)/shard_map/cond/branch_1_fun/ppermute | solution.py:457
  71.6 2.2 %restore.3 = f32[1024,256]{1,0:T(8,128)} custom-call(f32[1024,256]{1,0:T(8,128)S(1)} %get-tuple-element.154.spectra, bf16[1024,1024]{1,0:T(8,128)(2,1)S(1)} %get-tuple-element.155.back), custom_call_target="tpu_custom_call" | custom-call | flops 1073741824 | bytes 4194304 | tf_op jit(solution)/shard_map/cond/branch_1_fun/restore/pallas_call | solution.py:526
  73.8 0.6 collective-permute-done.12.from_below
  74.4 0.7 ocean.3
  (37 shorter events, 0.1 us)
Async XLA Ops:
  0.6 17.3 %copy-start = (bf16[128,1024]{1,0:T(8,128)(2,1)S(1)}, bf16[128,1024]{1,0:T(8,128)(2,1)}, u32[]{:S(2)}) copy-start(bf16[128,1024]{1,0:T(8,128)(2,1)} %stokes_table.1) | copy-start | bytes 786436
  0.6 17.3 %copy-start.1 = (s32[4,1024,2]{1,2,0:T(2,128)S(1)}, s32[4,1024,2]{1,2,0:T(2,128)}, u32[]{:S(2)}) copy-start(s32[4,1024,2]{1,2,0:T(2,128)} %param.22) | copy-start | bytes 98308
  0.7 17.3 %copy-start.2 = (f32[4,1024,2]{1,2,0:T(2,128)S(1)}, f32[4,1024,2]{1,2,0:T(2,128)}, u32[]{:S(2)}) copy-start(f32[4,1024,2]{1,2,0:T(2,128)} %param.23) | copy-start | bytes 98308
  0.7 17.2 %copy-start.3 = (f32[2,1024]{1,0:T(2,128)S(1)}, f32[2,1024]{1,0:T(2,128)}, u32[]{:S(2)}) copy-start(f32[2,1024]{1,0:T(2,128)} %courant.1) | copy-start | bytes 24580
  0.7 17.2 %copy-start.4 = (f32[1024]{0:T(1024)S(1)}, f32[1024]{0:T(1024)}, u32[]{:S(2)}) copy-start(f32[1024]{0:T(1024)} %param.24) | copy-start | bytes 12292
  0.7 17.2 %copy-start.5 = (s32[4,256]{1,0:T(4,128)S(1)}, s32[4,256]{1,0:T(4,128)}, u32[]{:S(2)}) copy-start(s32[4,256]{1,0:T(4,128)} %point_index.1) | copy-start | bytes 12292
  0.7 17.2 %copy-start.6 = (f32[4,256]{1,0:T(4,128)S(1)}, f32[4,256]{1,0:T(4,128)}, u32[]{:S(2)}) copy-start(f32[4,256]{1,0:T(4,128)} %point_weight.1) | copy-start | bytes 12292
  0.7 17.2 %copy-start.7 = (f32[64]{0:T(128)S(1)}, f32[64]{0:T(128)}, u32[]{:S(2)}) copy-start(f32[64]{0:T(128)} %param.32) | copy-start | bytes 772
  0.7 17.2 %copy-start.14 = (s32[2,1024]{1,0:T(2,128)S(1)}, s32[2,1024]{1,0:T(2,128)}, u32[]{:S(2)}) copy-start(s32[2,1024]{1,0:T(2,128)} %sign.3) | copy-start | bytes 24580
  0.7 17.2 %copy-start.15 = (f32[64]{0:T(128)S(1)}, f32[64]{0:T(128)}, u32[]{:S(2)}) copy-start(f32[64]{0:T(128)} %param.33) | copy-start | bytes 772
  3.7 28.2 %collective-permute-start.16 = (f32[632,256]{1,0:T(8,128)S(1)}, f32[632,256]{1,0:T(8,128)S(1)}, u32[]{:S(2)}, u32[]{:S(2)}) collective-permute-start(f32[632,256]{1,0:T(8,128)S(1)} %get-tuple-element.190.own_up), channel_id=1, source_target_pairs={{0,1},{1,2},{2,3},{3,4},{4,5},{5,6},{6,7},{7,8},{8,9},{9,10},{10,1... | collective-permute-start | bytes 1941512 | tf_op jit(solution)/shard_map/ppermute | solution.py:456
  6.3 25.6 %collective-permute-start.17 = (f32[632,256]{1,0:T(8,128)S(1)}, f32[632,256]{1,0:T(8,128)S(1)}, u32[]{:S(2)}, u32[]{:S(2)}) collective-permute-start(f32[632,256]{1,0:T(8,128)S(1)} %get-tuple-element.191.own_down), channel_id=1, source_target_pairs={{1,0},{2,1},{3,2},{4,3},{5,4},{6,5},{7,6},{8,7},{9,8},{10,9},{11,1... | collective-permute-start | bytes 1941512 | tf_op jit(solution)/shard_map/ppermute | solution.py:457
  15.5 15.8 %collective-permute-start.15 = (f32[64,128]{1,0:T(8,128)S(1)}, f32[64,128]{1,0:T(8,128)S(1)}, u32[]{:S(2)}, u32[]{:S(2)}) collective-permute-start(f32[64,128]{1,0:T(8,128)S(1)} %get-tuple-element.180), channel_id=1, source_target_pairs={{2,0},{3,1},{4,2},{5,3},{6,4},{7,5},{8,6},{9,7},{10,8},{11,9},{12,... | collective-permute-start | bytes 98312 | tf_op jit(solution)/shard_map/ppermute | solution.py:457
  17.9 14.0 %collective-permute-start.14 = (f32[64,128]{1,0:T(8,128)S(1)}, f32[64,128]{1,0:T(8,128)S(1)}, u32[]{:S(2)}, u32[]{:S(2)}) collective-permute-start(f32[64,128]{1,0:T(8,128)S(1)} %get-tuple-element.180), channel_id=1, source_target_pairs={{0,2},{1,3},{2,4},{3,5},{4,6},{5,7},{6,8},{7,9},{8,10},{9,11},{10,... | collective-permute-start | bytes 98312 | tf_op jit(solution)/shard_map/ppermute | solution.py:456
  25.5 6.4 %copy-start.8 = (f32[2,64,128]{2,1,0:T(8,128)S(1)}, f32[2,64,128]{2,1,0:T(8,128)}, u32[]{:S(2)}) copy-start(f32[2,64,128]{2,1,0:T(8,128)} %currents.1) | copy-start | bytes 196612
  25.5 6.4 %copy-start.9 = (f32[128]{0:T(128)S(1)}, f32[128]{0:T(128)}, u32[]{:S(2)}) copy-start(f32[128]{0:T(128)} %param.31) | copy-start | bytes 1540
  25.5 6.4 %copy-start.10 = (s32[256]{0:T(256)S(1)}, s32[256]{0:T(256)}, u32[]{:S(2)}) copy-start(s32[256]{0:T(256)} %param.19) | copy-start | bytes 3076
  25.5 6.4 %copy-start.11 = (s32[4,128]{1,0:T(4,128)S(1)}, s32[4,128]{1,0:T(4,128)}, u32[]{:S(2)}) copy-start(s32[4,128]{1,0:T(4,128)} %ocean_index.1) | copy-start | bytes 6148
  36.9 23.0 %collective-permute-start.8 = (f32[632,256]{1,0:T(8,128)S(1)}, f32[632,256]{1,0:T(8,128)S(1)}, u32[]{:S(2)}, u32[]{:S(2)}) collective-permute-start(f32[632,256]{1,0:T(8,128)S(1)} %get-tuple-element.146.own_up), channel_id=1, source_target_pairs={{0,1},{1,2},{2,3},{3,4},{4,5},{5,6},{6,7},{7,8},{8,9},{9,10},{10,1... | collective-permute-start | bytes 1941512 | tf_op jit(solution)/shard_map/cond/branch_1_fun/ppermute | solution.py:456
  37.0 22.9 %collective-permute-start.9 = (f32[632,256]{1,0:T(8,128)S(1)}, f32[632,256]{1,0:T(8,128)S(1)}, u32[]{:S(2)}, u32[]{:S(2)}) collective-permute-start(f32[632,256]{1,0:T(8,128)S(1)} %get-tuple-element.147.own_down), channel_id=1, source_target_pairs={{1,0},{2,1},{3,2},{4,3},{5,4},{6,5},{7,6},{8,7},{9,8},{10,9},{11,1... | collective-permute-start | bytes 1941512 | tf_op jit(solution)/shard_map/cond/branch_1_fun/ppermute | solution.py:457
  44.1 15.7 %collective-permute-start.10 = (f32[8,256]{1,0:T(8,128)S(1)}, f32[8,256]{1,0:T(8,128)S(1)}, u32[]{:S(2)}, u32[]{:S(2)}) collective-permute-start(f32[8,256]{1,0:T(8,128)S(1)} %get-tuple-element.148), channel_id=1, source_target_pairs={{0,2},{1,3},{2,4},{3,5},{4,6},{5,7},{6,8},{7,9},{8,10},{9,11},{10,... | collective-permute-start | bytes 24584 | tf_op jit(solution)/shard_map/cond/branch_1_fun/ppermute | solution.py:456
  44.1 15.7 %collective-permute-start.11 = (f32[8,256]{1,0:T(8,128)S(1)}, f32[8,256]{1,0:T(8,128)S(1)}, u32[]{:S(2)}, u32[]{:S(2)}) collective-permute-start(f32[8,256]{1,0:T(8,128)S(1)} %get-tuple-element.149), channel_id=1, source_target_pairs={{2,0},{3,1},{4,2},{5,3},{6,4},{7,5},{8,6},{9,7},{10,8},{11,9},{12,... | collective-permute-start | bytes 24584 | tf_op jit(solution)/shard_map/cond/branch_1_fun/ppermute | solution.py:457
  64.3 10.1 %collective-permute-start.12 = (f32[192,128]{1,0:T(8,128)S(1)}, f32[192,128]{1,0:T(8,128)S(1)}, u32[]{:S(2)}, u32[]{:S(2)}) collective-permute-start(f32[192,128]{1,0:T(8,128)S(1)} %get-tuple-element.157), channel_id=1, source_target_pairs={{0,1},{1,2},{2,3},{3,4},{4,5},{5,6},{6,7},{7,8},{8,9},{9,10},{10,1... | collective-permute-start | bytes 294920 | tf_op jit(solution)/shard_map/cond/branch_1_fun/ppermute | solution.py:456
  64.4 10.0 %collective-permute-start.13 = (f32[192,128]{1,0:T(8,128)S(1)}, f32[192,128]{1,0:T(8,128)S(1)}, u32[]{:S(2)}, u32[]{:S(2)}) collective-permute-start(f32[192,128]{1,0:T(8,128)S(1)} %get-tuple-element.158), channel_id=1, source_target_pairs={{1,0},{2,1},{3,2},{4,3},{5,4},{6,5},{7,6},{8,7},{9,8},{10,9},{11,1... | collective-permute-start | bytes 294920 | tf_op jit(solution)/shard_map/cond/branch_1_fun/ppermute | solution.py:457
  (2 other events, 12.8 us)

commit v2 on v1

--- a/solution.py
+++ b/solution.py
@@ -46,10 +46,11 @@
 
 
 def one_hot_rows(select_ref, pos_ref, copies=1):
-    place = lax.broadcasted_iota(jnp.int32, (K, 128), 0).astype(F32)
+    place = lax.broadcasted_iota(jnp.int16, (K, 128), 0)
     for block in range(8):
-        hit = place == pos_ref[block : block + 1, :]
-        ones = jnp.where(hit, 1.0, 0.0).astype(BF16)
+        line = pos_ref[block : block + 1, :].astype(jnp.int32)
+        line = jnp.broadcast_to(line, (16, 128)).astype(jnp.int16)[0:1]
+        ones = jnp.where(place == line, jnp.ones((), BF16), jnp.zeros((), BF16))
         for copy in range(copies):
             start = copy * K + block * 128
             select_ref[:, start : start + 128] = ones
@@ -205,7 +206,7 @@
 
 
 def update(count, own_up, own_down, from_below, from_above, flow, slope, quad, wide, stokes_sorted, wet,
-           advected, rounded, interp):
+           advected, rounded, finished):
     bend_x = jnp.tanh(flow[0])
     bend_y = jnp.tanh(flow[1])
     skip = K - count
@@ -244,26 +245,21 @@
     if skip:
         blocks(count, K, advect(own_down, skip, above))
 
-    def member(config, carry):
-        interp[config] = dot_nn(quad[config], rounded[...])
-        return carry
-
-    lax.fori_loop(0, 4, member, 0)
-
     def source(at, size):
-        at = pl.ds(at, size)
-        members = [interp[config, at, :] for config in range(4)]
-        value = advected[at, :]
+        rows = pl.ds(at, size)
+        members = [dot_nn(quad[config, rows, :], rounded[...]) for config in range(4)]
+        value = advected[rows, :]
         pairs = members[0] * members[1] + members[2] * members[3]
         total = (members[0] + members[1]) + (members[2] + members[3])
-        gain = wide[6, at, :]
+        gain = wide[6, rows, :]
         gain = jnp.concatenate([gain, gain], axis=1)
         result = wet * (value + gain * (value * (value * total - pairs)))
-        advected[at, :] = result
-        rounded[at, :] = result.astype(BF16)
-
-    blocks(0, K, source)
-    return dot_nn(stokes_sorted[...], rounded[...])
+        advected[rows, :] = result
+        finished[rows, :] = result.astype(BF16)
+
+    for at in range(0, K, 512):
+        source(at, 512)
+    return dot_nn(stokes_sorted[...], finished[...])
 
 
 def flow_of(sides, column, side, weight):
@@ -324,7 +320,7 @@
     count, row, own_up, own_down, from_below, from_above, below_two, above_two, surface, slope, quad, wide,
     stokes_sorted, cell_column, cell_side, cell_weight, wet, ocean_index, ocean_weight, currents,
     coriolis, mixing, level,
-    up, down, own_part, surface_part, far_up, far_down, cells, cells_low, advected, rounded, interp,
+    up, down, own_part, surface_part, far_up, far_down, cells, cells_low, advected, rounded, finished,
 ):
     base = row[0] * MX
     half = L // 2
@@ -344,7 +340,7 @@
     flow = flow_of(sides, cell_column, cell_side, cell_weight)
     wet_row = wet[...].astype(F32)
     stokes = update(count, own_up, own_down, from_below, from_above, flow, slope, quad, wide,
-                    stokes_sorted, wet_row, advected, rounded, interp)
+                    stokes_sorted, wet_row, advected, rounded, finished)
     up[0:count, :] = advected[0:count, :]
     down[0:count, :] = advected[K - count :, :]
     part = drift_parts(stokes, cells, cells_low)
@@ -387,7 +383,7 @@
     count, own_up, own_down, from_below, from_above, below_two, above_two, zonal_below, zonal_above,
     own_part, surface_part, slope, quad, wide, stokes_sorted, cell_column, cell_side, cell_weight, wet, cells,
     cells_low, currents, coriolis, mixing,
-    spectra, state, to_above, to_below, last_part, rounded, interp,
+    spectra, state, to_above, to_below, last_part, rounded, finished,
 ):
     half = L // 2
     below_extra = from_below[count:, :]
@@ -406,7 +402,7 @@
     state[1] = new_v
     wet_row = wet[...].astype(F32)
     stokes = update(count, own_up, own_down, from_below, from_above, flow, slope, quad, wide,
-                    stokes_sorted, wet_row, spectra, rounded, interp)
+                    stokes_sorted, wet_row, spectra, rounded, finished)
     part = drift_parts(stokes, cells, cells_low)
     to_below[0:128, :] = part[:, 0:OX]
     last_part[...] = part[:, OX : 2 * OX]
@@ -502,7 +498,7 @@
     message = shape(count + EXTRA, MX)
     far = shape(8, MX)
     table = shape(MX, 3 * OX, dtype=BF16)
-    work = (pltpu.VMEM((K, MX), BF16), pltpu.VMEM((4, K, MX), F32))
+    work = (pltpu.VMEM((K, MX), BF16), pltpu.VMEM((K, MX), BF16))
     next_up, next_down, own_part, surface_part, far_up, far_down, cells, cells_low = call(
         functools.partial(first_kernel, count),
         (message, message, part, far, far, far, table, table),

time: 75.2 us -> 73 us (0.971)
  Pallas kernels: 23.8 us -> 21.5 us
    pallas_call x1, Pallas kernels: 4.65 us -> 3.41 us  [steps(): call(functools.partial(first_kernel, count), (message, message, part, far...]
    pallas_call x1, Pallas kernels: 4.45 us -> 3.34 us  [steps(): call(functools.partial(second_kernel, count), (shape(K, MX), shape(2, L,...]
where the time goes in v2:
time: 73 us; the launch traced here: 72.9 us
  starting transfers between devices  36.7 us (50%)
  Pallas kernels  21.5 us (29%)
  waiting for transfers between devices  12.7 us (17%)
  between operations  1.54 us (2%)
    ppermute x5, starting transfers between devices, exchange(): lax.ppermute(to_below, AXES, [(b, a) for a, b in up])  34 us
    ppermute x5, waiting for transfers between devices, exchange(): lax.ppermute(to_above, AXES, up)  8.27 us
    pallas_call x1, Pallas kernels, tables(): call(table_kernel, (shape(4, K, K, dtype=BF16), shape(K, K, dtype=BF16),...  7.5 us
    ppermute x5, waiting for transfers between devices, exchange(): lax.ppermute(to_below, AXES, [(b, a) for a, b in up])  4.45 us
    pallas_call x1, Pallas kernels, steps(): call(functools.partial(first_kernel, count), (message, message, part, far...  3.41 us
    pallas_call x1, Pallas kernels, steps(): call(functools.partial(second_kernel, count), (shape(K, MX), shape(2, L,...  3.34 us
    pallas_call x1, Pallas kernels, pack(): call(functools.partial(pack_kernel, count), (message, message, shape(8, 1...  3.07 us
    ppermute x5, starting transfers between devices, exchange(): lax.ppermute(to_above, AXES, up)  2.74 us
  transfers between devices with their start and end apart: 10, of which 4 were waited for; matrix products, arithmetic and copies ran while one was open for 0% of the time, Pallas kernels for 15%

profile of v2, /device:TPU:1, one launch (start us, length us, event | category | flops | bytes accessed | tf_op | source)
XLA Modules:
  0.0 72.9 jit_solution(3969477515606483184)
XLA Ops:
  0.7 3.1 %pack.3 = (f32[632,256]{1,0:T(8,128)S(1)}, f32[632,256]{1,0:T(8,128)S(1)}, f32[8,128]{1,0:T(8,128)S(1)}, f32[8,128]{1,0:T(8,128)S(1)}, f32[64,128]{1,0:T(8,128)S(1)}, /*index=5*/s32[1]{0:T(128)}) custom-call(s32[2,1024]{1,0:T(2,128)} %sign.3, f32[1024,256]{1,0:T(8,128)} %spectrum.1, f32[2,64,128]{2,1,0:T(8,128)} %currents.1, f32[1,64]{1,0:T(1,128)} %bitcast.18, ...), custom_call_target="tpu_custom_call" | custom-call | flops 1610612736 | bytes 1048576 | tf_op jit(solution)/shard_map/pack/pallas_call | solution.py:459
  3.8 2.5 %collective-permute-start.16 = (f32[632,256]{1,0:T(8,128)S(1)}, f32[632,256]{1,0:T(8,128)S(1)}, u32[]{:S(2)}, u32[]{:S(2)}) collective-permute-start(f32[632,256]{1,0:T(8,128)S(1)} %get-tuple-element.190.own_up), channel_id=1, source_target_pairs={{0,1},{1,2},{2,3},{3,4},{4,5},{5,6},{6,7},{7,8},{8,9},{9,10},{10,1... | collective-permute-start | bytes 1941512 | tf_op jit(solution)/shard_map/ppermute | solution.py:452
  6.4 9.2 %collective-permute-start.17 = (f32[632,256]{1,0:T(8,128)S(1)}, f32[632,256]{1,0:T(8,128)S(1)}, u32[]{:S(2)}, u32[]{:S(2)}) collective-permute-start(f32[632,256]{1,0:T(8,128)S(1)} %get-tuple-element.191.own_down), channel_id=1, source_target_pairs={{1,0},{2,1},{3,2},{4,3},{5,4},{6,5},{7,6},{8,7},{9,8},{10,9},{11,1... | collective-permute-start | bytes 1941512 | tf_op jit(solution)/shard_map/ppermute | solution.py:453
  15.6 2.4 %collective-permute-start.15 = (f32[64,128]{1,0:T(8,128)S(1)}, f32[64,128]{1,0:T(8,128)S(1)}, u32[]{:S(2)}, u32[]{:S(2)}) collective-permute-start(f32[64,128]{1,0:T(8,128)S(1)} %get-tuple-element.180), channel_id=1, source_target_pairs={{2,0},{3,1},{4,2},{5,3},{6,4},{7,5},{8,6},{9,7},{10,8},{11,9},{12,... | collective-permute-start | bytes 98312 | tf_op jit(solution)/shard_map/ppermute | solution.py:453
  18.0 0.0 collective-permute-start.14
  18.1 7.5 %tables.1 = (bf16[4,1024,1024]{2,1,0:T(8,128)(2,1)S(1)}, bf16[1024,1024]{1,0:T(8,128)(2,1)S(1)}, bf16[128,1024]{1,0:T(8,128)(2,1)S(1)}, f32[7,1024,128]{2,1,0:T(...) custom-call(s32[1]{0:T(128)} %bitcast.3.row, ...), custom_call_target="tpu_custom_call" | custom-call | flops 4294967296 | bytes 12582912 | tf_op jit(solution)/shard_map/tables/pallas_call | solution.py:478
  25.6 0.0 copy-start.8
  25.6 0.0 copy-start.9
  25.6 0.6 slopes.7
  26.9 4.4 %collective-permute-done.15 = f32[64,128]{1,0:T(8,128)S(1)} collective-permute-done((f32[64,128]{1,0:T(8,128)S(1)}, f32[64,128]{1,0:T(8,128)S(1)}, u32[]{:S(2)}, u32[]{:S(2)}) %collective-permute-start.15) | collective-permute-done | bytes 32800 | tf_op jit(solution)/shard_map/ppermute | solution.py:453
  31.4 0.6 collective-permute-done.14
  32.1 40.8 %conditional.1 = (f32[1024,256]{1,0:T(8,128)}, f32[2,64,128]{2,1,0:T(8,128)}) conditional(s32[]{:T(128)} %bitcast.2, (s32[2,1024]{1,0:T(2,128)S(1)}, f32[1024,256]{1,0:T(8,128)S(1)}, f32[2,64,128]{2,1,0:T(8,128)S(1)}, f32[1,64]{1,0:T(1,128)S(1)}, f32[1,128]{1,0:T(1,128)S(1)}, /*index=5*/s32[4,128]{1,0:T(4,128)S(1)}, f32[4,128]{1,0:T(4,128)S(1)}, ...), branch_computations={%region_0.0_spmd, %region_1.0_spmd} | conditional | flops 11275337728 | bytes 57868624 | solution.py:565
  32.3 3.4 %first.3 = (f32[632,256]{1,0:T(8,128)S(1)}, f32[632,256]{1,0:T(8,128)S(1)}, f32[128,128]{1,0:T(8,128)S(1)}, f32[8,256]{1,0:T(8,128)S(1)}, f32[8,256]{1,0:T(8,128...) custom-call(s32[1]{0:T(128)} %get-tuple-element.124.row, ...), custom_call_target="tpu_custom_call" | custom-call | flops 3221225472 | bytes 12582912 | tf_op jit(solution)/shard_map/cond/branch_1_fun/first/pallas_call | solution.py:502
  35.7 0.1 collective-permute-start.8
  35.8 7.2 %collective-permute-start.9 = (f32[632,256]{1,0:T(8,128)S(1)}, f32[632,256]{1,0:T(8,128)S(1)}, u32[]{:S(2)}, u32[]{:S(2)}) collective-permute-start(f32[632,256]{1,0:T(8,128)S(1)} %get-tuple-element.147.own_down), channel_id=1, source_target_pairs={{1,0},{2,1},{3,2},{4,3},{5,4},{6,5},{7,6},{8,7},{9,8},{10,9},{11,1... | collective-permute-start | bytes 1941512 | tf_op jit(solution)/shard_map/cond/branch_1_fun/ppermute | solution.py:453
  43.0 8.1 %collective-permute-start.11 = (f32[8,256]{1,0:T(8,128)S(1)}, f32[8,256]{1,0:T(8,128)S(1)}, u32[]{:S(2)}, u32[]{:S(2)}) collective-permute-start(f32[8,256]{1,0:T(8,128)S(1)} %get-tuple-element.149), channel_id=1, source_target_pairs={{2,0},{3,1},{4,2},{5,3},{6,4},{7,5},{8,6},{9,7},{10,8},{11,9},{12,... | collective-permute-start | bytes 24584 | tf_op jit(solution)/shard_map/cond/branch_1_fun/ppermute | solution.py:453
  51.1 0.6 slopes.6.slope
  51.7 7.0 %collective-permute-done.10.below_two = f32[8,256]{1,0:T(8,128)S(1)} collective-permute-done((f32[8,256]{1,0:T(8,128)S(1)}, f32[8,256]{1,0:T(8,128)S(1)}, u32[]{:S(2)}, u32[]{:S(2)}) %collective-permute-start.10) | collective-permute-done | bytes 8224 | tf_op jit(solution)/shard_map/cond/branch_1_fun/ppermute | solution.py:452
  58.7 3.3 %second.3 = (f32[1024,256]{1,0:T(8,128)S(1)}, f32[2,64,128]{2,1,0:T(8,128)S(1)}, f32[192,128]{1,0:T(8,128)S(1)}, f32[192,128]{1,0:T(8,128)S(1)}, f32[128,128]{1,0:T(8,128)S(1)}) custom-call(f32[632,256]{1,0:T(8,128)S(1)} %get-tuple-element.146.own_up, f32[632,256]{1,0:T(8,128)S(1)} %get-tuple-element.147.own_down, ...), custom_call_target="tpu_custom_call" | custom-call | flops 3221225472 | bytes 12582912 | tf_op jit(solution)/shard_map/cond/branch_1_fun/second/pallas_call | solution.py:514
  62.1 0.1 collective-permute-start.12
  62.1 7.2 %collective-permute-start.13 = (f32[192,128]{1,0:T(8,128)S(1)}, f32[192,128]{1,0:T(8,128)S(1)}, u32[]{:S(2)}, u32[]{:S(2)}) collective-permute-start(f32[192,128]{1,0:T(8,128)S(1)} %get-tuple-element.158), channel_id=1, source_target_pairs={{1,0},{2,1},{3,2},{4,3},{5,4},{6,5},{7,6},{8,7},{9,8},{10,9},{11,1... | collective-permute-start | bytes 294920 | tf_op jit(solution)/shard_map/cond/branch_1_fun/ppermute | solution.py:453
  69.3 2.2 %restore.3 = f32[1024,256]{1,0:T(8,128)} custom-call(f32[1024,256]{1,0:T(8,128)S(1)} %get-tuple-element.154.spectra, bf16[1024,1024]{1,0:T(8,128)(2,1)S(1)} %get-tuple-element.155.back), custom_call_target="tpu_custom_call" | custom-call | flops 1073741824 | bytes 4194304 | tf_op jit(solution)/shard_map/cond/branch_1_fun/restore/pallas_call | solution.py:522
  71.5 0.6 collective-permute-done.12.from_below
  72.1 0.7 ocean.3
  (37 shorter events, 0.1 us)
Async XLA Ops:
  0.6 17.4 %copy-start = (bf16[128,1024]{1,0:T(8,128)(2,1)S(1)}, bf16[128,1024]{1,0:T(8,128)(2,1)}, u32[]{:S(2)}) copy-start(bf16[128,1024]{1,0:T(8,128)(2,1)} %stokes_table.1) | copy-start | bytes 786436
  0.6 17.4 %copy-start.1 = (s32[4,1024,2]{1,2,0:T(2,128)S(1)}, s32[4,1024,2]{1,2,0:T(2,128)}, u32[]{:S(2)}) copy-start(s32[4,1024,2]{1,2,0:T(2,128)} %param.22) | copy-start | bytes 98308
  0.7 17.3 %copy-start.2 = (f32[4,1024,2]{1,2,0:T(2,128)S(1)}, f32[4,1024,2]{1,2,0:T(2,128)}, u32[]{:S(2)}) copy-start(f32[4,1024,2]{1,2,0:T(2,128)} %param.23) | copy-start | bytes 98308
  0.7 17.3 %copy-start.3 = (f32[2,1024]{1,0:T(2,128)S(1)}, f32[2,1024]{1,0:T(2,128)}, u32[]{:S(2)}) copy-start(f32[2,1024]{1,0:T(2,128)} %courant.1) | copy-start | bytes 24580
  0.7 17.3 %copy-start.4 = (f32[1024]{0:T(1024)S(1)}, f32[1024]{0:T(1024)}, u32[]{:S(2)}) copy-start(f32[1024]{0:T(1024)} %param.24) | copy-start | bytes 12292
  0.7 17.3 %copy-start.5 = (s32[4,256]{1,0:T(4,128)S(1)}, s32[4,256]{1,0:T(4,128)}, u32[]{:S(2)}) copy-start(s32[4,256]{1,0:T(4,128)} %point_index.1) | copy-start | bytes 12292
  0.7 17.3 %copy-start.6 = (f32[4,256]{1,0:T(4,128)S(1)}, f32[4,256]{1,0:T(4,128)}, u32[]{:S(2)}) copy-start(f32[4,256]{1,0:T(4,128)} %point_weight.1) | copy-start | bytes 12292
  0.7 17.3 %copy-start.7 = (f32[64]{0:T(128)S(1)}, f32[64]{0:T(128)}, u32[]{:S(2)}) copy-start(f32[64]{0:T(128)} %param.32) | copy-start | bytes 772
  0.7 17.3 %copy-start.14 = (s32[2,1024]{1,0:T(2,128)S(1)}, s32[2,1024]{1,0:T(2,128)}, u32[]{:S(2)}) copy-start(s32[2,1024]{1,0:T(2,128)} %sign.3) | copy-start | bytes 24580
  0.7 17.3 %copy-start.15 = (f32[64]{0:T(128)S(1)}, f32[64]{0:T(128)}, u32[]{:S(2)}) copy-start(f32[64]{0:T(128)} %param.33) | copy-start | bytes 772
  3.8 28.2 %collective-permute-start.16 = (f32[632,256]{1,0:T(8,128)S(1)}, f32[632,256]{1,0:T(8,128)S(1)}, u32[]{:S(2)}, u32[]{:S(2)}) collective-permute-start(f32[632,256]{1,0:T(8,128)S(1)} %get-tuple-element.190.own_up), channel_id=1, source_target_pairs={{0,1},{1,2},{2,3},{3,4},{4,5},{5,6},{6,7},{7,8},{8,9},{9,10},{10,1... | collective-permute-start | bytes 1941512 | tf_op jit(solution)/shard_map/ppermute | solution.py:452
  6.4 25.6 %collective-permute-start.17 = (f32[632,256]{1,0:T(8,128)S(1)}, f32[632,256]{1,0:T(8,128)S(1)}, u32[]{:S(2)}, u32[]{:S(2)}) collective-permute-start(f32[632,256]{1,0:T(8,128)S(1)} %get-tuple-element.191.own_down), channel_id=1, source_target_pairs={{1,0},{2,1},{3,2},{4,3},{5,4},{6,5},{7,6},{8,7},{9,8},{10,9},{11,1... | collective-permute-start | bytes 1941512 | tf_op jit(solution)/shard_map/ppermute | solution.py:453
  15.6 15.8 %collective-permute-start.15 = (f32[64,128]{1,0:T(8,128)S(1)}, f32[64,128]{1,0:T(8,128)S(1)}, u32[]{:S(2)}, u32[]{:S(2)}) collective-permute-start(f32[64,128]{1,0:T(8,128)S(1)} %get-tuple-element.180), channel_id=1, source_target_pairs={{2,0},{3,1},{4,2},{5,3},{6,4},{7,5},{8,6},{9,7},{10,8},{11,9},{12,... | collective-permute-start | bytes 98312 | tf_op jit(solution)/shard_map/ppermute | solution.py:453
  18.0 14.0 %collective-permute-start.14 = (f32[64,128]{1,0:T(8,128)S(1)}, f32[64,128]{1,0:T(8,128)S(1)}, u32[]{:S(2)}, u32[]{:S(2)}) collective-permute-start(f32[64,128]{1,0:T(8,128)S(1)} %get-tuple-element.180), channel_id=1, source_target_pairs={{0,2},{1,3},{2,4},{3,5},{4,6},{5,7},{6,8},{7,9},{8,10},{9,11},{10,... | collective-permute-start | bytes 98312 | tf_op jit(solution)/shard_map/ppermute | solution.py:452
  25.6 6.4 %copy-start.8 = (f32[2,64,128]{2,1,0:T(8,128)S(1)}, f32[2,64,128]{2,1,0:T(8,128)}, u32[]{:S(2)}) copy-start(f32[2,64,128]{2,1,0:T(8,128)} %currents.1) | copy-start | bytes 196612
  25.6 6.4 %copy-start.9 = (f32[128]{0:T(128)S(1)}, f32[128]{0:T(128)}, u32[]{:S(2)}) copy-start(f32[128]{0:T(128)} %param.31) | copy-start | bytes 1540
  25.6 6.4 %copy-start.10 = (s32[256]{0:T(256)S(1)}, s32[256]{0:T(256)}, u32[]{:S(2)}) copy-start(s32[256]{0:T(256)} %param.19) | copy-start | bytes 3076
  25.6 6.4 %copy-start.11 = (s32[4,128]{1,0:T(4,128)S(1)}, s32[4,128]{1,0:T(4,128)}, u32[]{:S(2)}) copy-start(s32[4,128]{1,0:T(4,128)} %ocean_index.1) | copy-start | bytes 6148
  35.7 23.0 %collective-permute-start.8 = (f32[632,256]{1,0:T(8,128)S(1)}, f32[632,256]{1,0:T(8,128)S(1)}, u32[]{:S(2)}, u32[]{:S(2)}) collective-permute-start(f32[632,256]{1,0:T(8,128)S(1)} %get-tuple-element.146.own_up), channel_id=1, source_target_pairs={{0,1},{1,2},{2,3},{3,4},{4,5},{5,6},{6,7},{7,8},{8,9},{9,10},{10,1... | collective-permute-start | bytes 1941512 | tf_op jit(solution)/shard_map/cond/branch_1_fun/ppermute | solution.py:452
  35.8 22.9 %collective-permute-start.9 = (f32[632,256]{1,0:T(8,128)S(1)}, f32[632,256]{1,0:T(8,128)S(1)}, u32[]{:S(2)}, u32[]{:S(2)}) collective-permute-start(f32[632,256]{1,0:T(8,128)S(1)} %get-tuple-element.147.own_down), channel_id=1, source_target_pairs={{1,0},{2,1},{3,2},{4,3},{5,4},{6,5},{7,6},{8,7},{9,8},{10,9},{11,1... | collective-permute-start | bytes 1941512 | tf_op jit(solution)/shard_map/cond/branch_1_fun/ppermute | solution.py:453
  43.0 15.7 %collective-permute-start.10 = (f32[8,256]{1,0:T(8,128)S(1)}, f32[8,256]{1,0:T(8,128)S(1)}, u32[]{:S(2)}, u32[]{:S(2)}) collective-permute-start(f32[8,256]{1,0:T(8,128)S(1)} %get-tuple-element.148), channel_id=1, source_target_pairs={{0,2},{1,3},{2,4},{3,5},{4,6},{5,7},{6,8},{7,9},{8,10},{9,11},{10,... | collective-permute-start | bytes 24584 | tf_op jit(solution)/shard_map/cond/branch_1_fun/ppermute | solution.py:452
  43.0 15.7 %collective-permute-start.11 = (f32[8,256]{1,0:T(8,128)S(1)}, f32[8,256]{1,0:T(8,128)S(1)}, u32[]{:S(2)}, u32[]{:S(2)}) collective-permute-start(f32[8,256]{1,0:T(8,128)S(1)} %get-tuple-element.149), channel_id=1, source_target_pairs={{2,0},{3,1},{4,2},{5,3},{6,4},{7,5},{8,6},{9,7},{10,8},{11,9},{12,... | collective-permute-start | bytes 24584 | tf_op jit(solution)/shard_map/cond/branch_1_fun/ppermute | solution.py:453
  62.1 10.1 %collective-permute-start.12 = (f32[192,128]{1,0:T(8,128)S(1)}, f32[192,128]{1,0:T(8,128)S(1)}, u32[]{:S(2)}, u32[]{:S(2)}) collective-permute-start(f32[192,128]{1,0:T(8,128)S(1)} %get-tuple-element.157), channel_id=1, source_target_pairs={{0,1},{1,2},{2,3},{3,4},{4,5},{5,6},{6,7},{7,8},{8,9},{9,10},{10,1... | collective-permute-start | bytes 294920 | tf_op jit(solution)/shard_map/cond/branch_1_fun/ppermute | solution.py:452
  62.1 10.0 %collective-permute-start.13 = (f32[192,128]{1,0:T(8,128)S(1)}, f32[192,128]{1,0:T(8,128)S(1)}, u32[]{:S(2)}, u32[]{:S(2)}) collective-permute-start(f32[192,128]{1,0:T(8,128)S(1)} %get-tuple-element.158), channel_id=1, source_target_pairs={{1,0},{2,1},{3,2},{4,3},{5,4},{6,5},{7,6},{8,7},{9,8},{10,9},{11,1... | collective-permute-start | bytes 294920 | tf_op jit(solution)/shard_map/cond/branch_1_fun/ppermute | solution.py:453
  (2 other events, 12.8 us)

commit v3 on v2

--- a/solution.py
+++ b/solution.py
@@ -63,30 +63,30 @@
     for block in range(8):
         pos[block : block + 1, :] = sign[1:2, block * 128 : (block + 1) * 128].astype(F32)
     ones = pos[...]
-    upper = lax.broadcasted_iota(jnp.int32, (128, 128), 0) <= lax.broadcasted_iota(
-        jnp.int32, (128, 128), 1
-    )
-    before = dot_nn(ones.astype(BF16), jnp.where(upper, 1.0, 0.0).astype(BF16))
-    running = jnp.zeros((1, 1), F32)
-    counts = []
-    for block in range(8):
-        counts.append(before[block : block + 1, :] + running)
-        running = running + before[block : block + 1, 127:128]
-    northward = jnp.sum(running)
-    fits[0] = jnp.logical_and(northward <= count, K - northward <= count).astype(jnp.int32)
-    lane = lax.broadcasted_iota(jnp.int32, (1, 128), 1).astype(F32)
-    for block in range(8):
-        index = lane + float(block * 128)
-        first = counts[block] - 1.0
-        second = running + index - counts[block]
-        pos[block : block + 1, :] = jnp.where(ones[block : block + 1, :] > 0.5, first, second)
-    one_hot_rows(select, pos, 2)
+    upper = lax.broadcasted_iota(jnp.int32, (128, 256), 0) <= lax.broadcasted_iota(
+        jnp.int32, (128, 256), 1
+    )
+    sums = dot_nn(ones.astype(BF16), jnp.where(upper, 1.0, 0.0).astype(BF16))
+    in_line, total = sums[:, 0:128], sums[:, 128:]
+    line = lax.broadcasted_iota(jnp.int32, (8, 128), 0)
+    running = total
+    northward = total
+    for shift in (1, 2, 4):
+        running = running + jnp.where(line >= shift, pltpu.roll(running, shift, 0), 0.0)
+        northward = northward + pltpu.roll(northward, shift, 0)
+    before = in_line + (running - total)
+    index = (line * 128 + lax.broadcasted_iota(jnp.int32, (8, 128), 1)).astype(F32)
+    pos[...] = jnp.where(ones > 0.5, before - 1.0, northward + index - before)
+    one_hot_rows(select, pos)
     high, low = split2(spectrum[...])
-    parts[0:K, :] = low
-    parts[K:, :] = high
-    value = dot_nn(select[...], parts[...])
+    parts[:, 0:MX] = low
+    parts[:, MX:] = high
+    both = dot_nn(select[...], parts[...])
+    value = both[:, 0:MX] + both[:, MX:]
     up[0:count, :] = value[0:count, :]
     down[0:count, :] = value[K - count :, :]
+    some = jnp.sum(northward[0:1, 0:1])
+    fits[0] = jnp.logical_and(some <= count, K - some <= count).astype(jnp.int32)
     weights = jnp.broadcast_to(level[...], (8, L))
     flat_u = dot_exact(weights, currents[0])
     flat_v = dot_exact(weights, currents[1])
@@ -206,7 +206,7 @@
 
 
 def update(count, own_up, own_down, from_below, from_above, flow, slope, quad, wide, stokes_sorted, wet,
-           advected, rounded, finished):
+           write, advected, rounded, finished):
     bend_x = jnp.tanh(flow[0])
     bend_y = jnp.tanh(flow[1])
     skip = K - count
@@ -254,7 +254,7 @@
         gain = wide[6, rows, :]
         gain = jnp.concatenate([gain, gain], axis=1)
         result = wet * (value + gain * (value * (value * total - pairs)))
-        advected[rows, :] = result
+        write(at, size, result)
         finished[rows, :] = result.astype(BF16)
 
     for at in range(0, K, 512):
@@ -339,10 +339,17 @@
     sides = (below_extra[0:1, :], own, above_extra[0:1, :])
     flow = flow_of(sides, cell_column, cell_side, cell_weight)
     wet_row = wet[...].astype(F32)
+
+    def write(at, size, result):
+        top = min(at + size, count)
+        if top > at:
+            up[at:top, :] = result[0 : top - at]
+        start = max(at, K - count)
+        if start < at + size:
+            down[start - K + count : at + size - K + count, :] = result[start - at :]
+
     stokes = update(count, own_up, own_down, from_below, from_above, flow, slope, quad, wide,
-                    stokes_sorted, wet_row, advected, rounded, finished)
-    up[0:count, :] = advected[0:count, :]
-    down[0:count, :] = advected[K - count :, :]
+                    stokes_sorted, wet_row, write, advected, rounded, finished)
     part = drift_parts(stokes, cells, cells_low)
     u, v = currents[0], currents[1]
     u_below, v_below = tall(below_extra[8 : 8 + half]), tall(below_extra[8 + half : 8 + 2 * half])
@@ -401,8 +408,12 @@
     state[0] = new_u
     state[1] = new_v
     wet_row = wet[...].astype(F32)
+
+    def write(at, size, result):
+        spectra[at : at + size, :] = result
+
     stokes = update(count, own_up, own_down, from_below, from_above, flow, slope, quad, wide,
-                    stokes_sorted, wet_row, spectra, rounded, finished)
+                    stokes_sorted, wet_row, write, spectra, rounded, finished)
     part = drift_parts(stokes, cells, cells_low)
     to_below[0:128, :] = part[:, 0:OX]
     last_part[...] = part[:, OX : 2 * OX]
@@ -459,7 +470,7 @@
     return call(
         functools.partial(pack_kernel, count),
         (message, message, shape(8, 128), shape(8, 128), shape(L, OX), shape(1, dtype=jnp.int32)),
-        (pltpu.VMEM((K, 2 * K), BF16), pltpu.VMEM((2 * K, MX), BF16)),
+        (pltpu.VMEM((K, K), BF16), pltpu.VMEM((K, 2 * MX), BF16)),
         inputs=7, flops=2 * K * K * 3 * MX, data=1 << 20, name="pack",
         out_specs=(VMEM, VMEM, VMEM, VMEM, VMEM, SMEM),
     )(stencil_sign, spectrum, currents, level, coriolis, ocean_index, ocean_weight)

time: 73 us -> 72.7 us (level)
  no operation moved by 1% of the time
where the time goes in v3:
time: 72.7 us; the launch traced here: 72.6 us
  starting transfers between devices  36.8 us (51%)
  Pallas kernels  21.2 us (29%)
  waiting for transfers between devices  12.7 us (17%)
  between operations  1.54 us (2%)
    ppermute x5, starting transfers between devices, exchange(): lax.ppermute(to_below, AXES, [(b, a) for a, b in up])  34 us
    ppermute x5, waiting for transfers between devices, exchange(): lax.ppermute(to_above, AXES, up)  8.27 us
    pallas_call x1, Pallas kernels, tables(): call(table_kernel, (shape(4, K, K, dtype=BF16), shape(K, K, dtype=BF16),...  7.5 us
    ppermute x5, waiting for transfers between devices, exchange(): lax.ppermute(to_below, AXES, [(b, a) for a, b in up])  4.45 us
    pallas_call x1, Pallas kernels, steps(): call(functools.partial(first_kernel, count), (message, message, part, far...  3.42 us
    pallas_call x1, Pallas kernels, steps(): call(functools.partial(second_kernel, count), (shape(K, MX), shape(2, L,...  3.35 us
    pallas_call x1, Pallas kernels, pack(): call(functools.partial(pack_kernel, count), (message, message, shape(8, 1...  2.8 us
    ppermute x5, starting transfers between devices, exchange(): lax.ppermute(to_above, AXES, up)  2.74 us
  transfers between devices with their start and end apart: 10, of which 4 were waited for; matrix products, arithmetic and copies ran while one was open for 0% of the time, Pallas kernels for 15%

profile of v3, /device:TPU:1, one launch (start us, length us, event | category | flops | bytes accessed | tf_op | source)
XLA Modules:
  0.0 72.6 jit_solution(17642496031809946315)
XLA Ops:
  0.7 2.8 %pack.3 = (f32[632,256]{1,0:T(8,128)S(1)}, f32[632,256]{1,0:T(8,128)S(1)}, f32[8,128]{1,0:T(8,128)S(1)}, f32[8,128]{1,0:T(8,128)S(1)}, f32[64,128]{1,0:T(8,128)S(1)}, /*index=5*/s32[1]{0:T(128)}) custom-call(s32[2,1024]{1,0:T(2,128)} %sign.3, f32[1024,256]{1,0:T(8,128)} %spectrum.1, f32[2,64,128]{2,1,0:T(8,128)} %currents.1, f32[1,64]{1,0:T(1,128)} %bitcast.18, ...), custom_call_target="tpu_custom_call" | custom-call | flops 1610612736 | bytes 1048576 | tf_op jit(solution)/shard_map/pack/pallas_call | solution.py:470
  3.5 2.5 %collective-permute-start.16 = (f32[632,256]{1,0:T(8,128)S(1)}, f32[632,256]{1,0:T(8,128)S(1)}, u32[]{:S(2)}, u32[]{:S(2)}) collective-permute-start(f32[632,256]{1,0:T(8,128)S(1)} %get-tuple-element.190.own_up), channel_id=1, source_target_pairs={{0,1},{1,2},{2,3},{3,4},{4,5},{5,6},{6,7},{7,8},{8,9},{9,10},{10,1... | collective-permute-start | bytes 1941512 | tf_op jit(solution)/shard_map/ppermute | solution.py:463
  6.1 9.2 %collective-permute-start.17 = (f32[632,256]{1,0:T(8,128)S(1)}, f32[632,256]{1,0:T(8,128)S(1)}, u32[]{:S(2)}, u32[]{:S(2)}) collective-permute-start(f32[632,256]{1,0:T(8,128)S(1)} %get-tuple-element.191.own_down), channel_id=1, source_target_pairs={{1,0},{2,1},{3,2},{4,3},{5,4},{6,5},{7,6},{8,7},{9,8},{10,9},{11,1... | collective-permute-start | bytes 1941512 | tf_op jit(solution)/shard_map/ppermute | solution.py:464
  15.3 2.4 %collective-permute-start.15 = (f32[64,128]{1,0:T(8,128)S(1)}, f32[64,128]{1,0:T(8,128)S(1)}, u32[]{:S(2)}, u32[]{:S(2)}) collective-permute-start(f32[64,128]{1,0:T(8,128)S(1)} %get-tuple-element.180), channel_id=1, source_target_pairs={{2,0},{3,1},{4,2},{5,3},{6,4},{7,5},{8,6},{9,7},{10,8},{11,9},{12,... | collective-permute-start | bytes 98312 | tf_op jit(solution)/shard_map/ppermute | solution.py:464
  17.7 0.0 collective-permute-start.14
  17.8 7.5 %tables.1 = (bf16[4,1024,1024]{2,1,0:T(8,128)(2,1)S(1)}, bf16[1024,1024]{1,0:T(8,128)(2,1)S(1)}, bf16[128,1024]{1,0:T(8,128)(2,1)S(1)}, f32[7,1024,128]{2,1,0:T(...) custom-call(s32[1]{0:T(128)} %bitcast.3.row, ...), custom_call_target="tpu_custom_call" | custom-call | flops 4294967296 | bytes 12582912 | tf_op jit(solution)/shard_map/tables/pallas_call | solution.py:489
  25.3 0.0 copy-start.8
  25.3 0.0 copy-start.11
  25.4 0.6 slopes.7
  26.7 4.4 %collective-permute-done.15 = f32[64,128]{1,0:T(8,128)S(1)} collective-permute-done((f32[64,128]{1,0:T(8,128)S(1)}, f32[64,128]{1,0:T(8,128)S(1)}, u32[]{:S(2)}, u32[]{:S(2)}) %collective-permute-start.15) | collective-permute-done | bytes 32800 | tf_op jit(solution)/shard_map/ppermute | solution.py:464
  31.1 0.6 collective-permute-done.14
  31.8 40.8 %conditional.1 = (f32[1024,256]{1,0:T(8,128)}, f32[2,64,128]{2,1,0:T(8,128)}) conditional(s32[]{:T(128)} %bitcast.2, (s32[2,1024]{1,0:T(2,128)S(1)}, f32[1024,256]{1,0:T(8,128)S(1)}, f32[2,64,128]{2,1,0:T(8,128)S(1)}, f32[1,64]{1,0:T(1,128)S(1)}, f32[1,128]{1,0:T(1,128)S(1)}, /*index=5*/s32[4,128]{1,0:T(4,128)S(1)}, f32[4,128]{1,0:T(4,128)S(1)}, ...), branch_computations={%region_0.0_spmd, %region_1.0_spmd} | conditional | flops 11275337728 | bytes 57868624 | solution.py:576
  32.0 3.4 %first.3 = (f32[632,256]{1,0:T(8,128)S(1)}, f32[632,256]{1,0:T(8,128)S(1)}, f32[128,128]{1,0:T(8,128)S(1)}, f32[8,256]{1,0:T(8,128)S(1)}, f32[8,256]{1,0:T(8,128...) custom-call(s32[1]{0:T(128)} %get-tuple-element.124.row, ...), custom_call_target="tpu_custom_call" | custom-call | flops 3221225472 | bytes 12582912 | tf_op jit(solution)/shard_map/cond/branch_1_fun/first/pallas_call | solution.py:513
  35.4 0.1 collective-permute-start.8
  35.5 7.2 %collective-permute-start.9 = (f32[632,256]{1,0:T(8,128)S(1)}, f32[632,256]{1,0:T(8,128)S(1)}, u32[]{:S(2)}, u32[]{:S(2)}) collective-permute-start(f32[632,256]{1,0:T(8,128)S(1)} %get-tuple-element.147.own_down), channel_id=1, source_target_pairs={{1,0},{2,1},{3,2},{4,3},{5,4},{6,5},{7,6},{8,7},{9,8},{10,9},{11,1... | collective-permute-start | bytes 1941512 | tf_op jit(solution)/shard_map/cond/branch_1_fun/ppermute | solution.py:464
  42.7 8.1 %collective-permute-start.11 = (f32[8,256]{1,0:T(8,128)S(1)}, f32[8,256]{1,0:T(8,128)S(1)}, u32[]{:S(2)}, u32[]{:S(2)}) collective-permute-start(f32[8,256]{1,0:T(8,128)S(1)} %get-tuple-element.149), channel_id=1, source_target_pairs={{2,0},{3,1},{4,2},{5,3},{6,4},{7,5},{8,6},{9,7},{10,8},{11,9},{12,... | collective-permute-start | bytes 24584 | tf_op jit(solution)/shard_map/cond/branch_1_fun/ppermute | solution.py:464
  50.8 0.6 slopes.6.slope
  51.4 7.0 %collective-permute-done.10.below_two = f32[8,256]{1,0:T(8,128)S(1)} collective-permute-done((f32[8,256]{1,0:T(8,128)S(1)}, f32[8,256]{1,0:T(8,128)S(1)}, u32[]{:S(2)}, u32[]{:S(2)}) %collective-permute-start.10) | collective-permute-done | bytes 8224 | tf_op jit(solution)/shard_map/cond/branch_1_fun/ppermute | solution.py:463
  58.4 3.3 %second.3 = (f32[1024,256]{1,0:T(8,128)S(1)}, f32[2,64,128]{2,1,0:T(8,128)S(1)}, f32[192,128]{1,0:T(8,128)S(1)}, f32[192,128]{1,0:T(8,128)S(1)}, f32[128,128]{1,0:T(8,128)S(1)}) custom-call(f32[632,256]{1,0:T(8,128)S(1)} %get-tuple-element.146.own_up, f32[632,256]{1,0:T(8,128)S(1)} %get-tuple-element.147.own_down, ...), custom_call_target="tpu_custom_call" | custom-call | flops 3221225472 | bytes 12582912 | tf_op jit(solution)/shard_map/cond/branch_1_fun/second/pallas_call | solution.py:525
  61.8 0.1 collective-permute-start.12
  61.9 7.2 %collective-permute-start.13 = (f32[192,128]{1,0:T(8,128)S(1)}, f32[192,128]{1,0:T(8,128)S(1)}, u32[]{:S(2)}, u32[]{:S(2)}) collective-permute-start(f32[192,128]{1,0:T(8,128)S(1)} %get-tuple-element.158), channel_id=1, source_target_pairs={{1,0},{2,1},{3,2},{4,3},{5,4},{6,5},{7,6},{8,7},{9,8},{10,9},{11,1... | collective-permute-start | bytes 294920 | tf_op jit(solution)/shard_map/cond/branch_1_fun/ppermute | solution.py:464
  69.0 2.2 %restore.3 = f32[1024,256]{1,0:T(8,128)} custom-call(f32[1024,256]{1,0:T(8,128)S(1)} %get-tuple-element.154.spectra, bf16[1024,1024]{1,0:T(8,128)(2,1)S(1)} %get-tuple-element.155.back), custom_call_target="tpu_custom_call" | custom-call | flops 1073741824 | bytes 4194304 | tf_op jit(solution)/shard_map/cond/branch_1_fun/restore/pallas_call | solution.py:533
  71.3 0.6 collective-permute-done.12.from_below
  71.9 0.7 ocean.3
  (37 shorter events, 0.1 us)
Async XLA Ops:
  0.6 17.1 %copy-start = (bf16[128,1024]{1,0:T(8,128)(2,1)S(1)}, bf16[128,1024]{1,0:T(8,128)(2,1)}, u32[]{:S(2)}) copy-start(bf16[128,1024]{1,0:T(8,128)(2,1)} %stokes_table.1) | copy-start | bytes 786436
  0.6 17.1 %copy-start.1 = (s32[4,1024,2]{1,2,0:T(2,128)S(1)}, s32[4,1024,2]{1,2,0:T(2,128)}, u32[]{:S(2)}) copy-start(s32[4,1024,2]{1,2,0:T(2,128)} %param.22) | copy-start | bytes 98308
  0.7 17.1 %copy-start.2 = (f32[4,1024,2]{1,2,0:T(2,128)S(1)}, f32[4,1024,2]{1,2,0:T(2,128)}, u32[]{:S(2)}) copy-start(f32[4,1024,2]{1,2,0:T(2,128)} %param.23) | copy-start | bytes 98308
  0.7 17.1 %copy-start.3 = (f32[2,1024]{1,0:T(2,128)S(1)}, f32[2,1024]{1,0:T(2,128)}, u32[]{:S(2)}) copy-start(f32[2,1024]{1,0:T(2,128)} %courant.1) | copy-start | bytes 24580
  0.7 17.1 %copy-start.4 = (f32[1024]{0:T(1024)S(1)}, f32[1024]{0:T(1024)}, u32[]{:S(2)}) copy-start(f32[1024]{0:T(1024)} %param.24) | copy-start | bytes 12292
  0.7 17.1 %copy-start.5 = (s32[4,256]{1,0:T(4,128)S(1)}, s32[4,256]{1,0:T(4,128)}, u32[]{:S(2)}) copy-start(s32[4,256]{1,0:T(4,128)} %point_index.1) | copy-start | bytes 12292
  0.7 17.1 %copy-start.6 = (f32[4,256]{1,0:T(4,128)S(1)}, f32[4,256]{1,0:T(4,128)}, u32[]{:S(2)}) copy-start(f32[4,256]{1,0:T(4,128)} %point_weight.1) | copy-start | bytes 12292
  0.7 17.1 %copy-start.7 = (f32[64]{0:T(128)S(1)}, f32[64]{0:T(128)}, u32[]{:S(2)}) copy-start(f32[64]{0:T(128)} %param.32) | copy-start | bytes 772
  0.7 17.1 %copy-start.14 = (s32[2,1024]{1,0:T(2,128)S(1)}, s32[2,1024]{1,0:T(2,128)}, u32[]{:S(2)}) copy-start(s32[2,1024]{1,0:T(2,128)} %sign.3) | copy-start | bytes 24580
  0.7 17.1 %copy-start.15 = (f32[64]{0:T(128)S(1)}, f32[64]{0:T(128)}, u32[]{:S(2)}) copy-start(f32[64]{0:T(128)} %param.33) | copy-start | bytes 772
  3.5 28.2 %collective-permute-start.16 = (f32[632,256]{1,0:T(8,128)S(1)}, f32[632,256]{1,0:T(8,128)S(1)}, u32[]{:S(2)}, u32[]{:S(2)}) collective-permute-start(f32[632,256]{1,0:T(8,128)S(1)} %get-tuple-element.190.own_up), channel_id=1, source_target_pairs={{0,1},{1,2},{2,3},{3,4},{4,5},{5,6},{6,7},{7,8},{8,9},{9,10},{10,1... | collective-permute-start | bytes 1941512 | tf_op jit(solution)/shard_map/ppermute | solution.py:463
  6.1 25.6 %collective-permute-start.17 = (f32[632,256]{1,0:T(8,128)S(1)}, f32[632,256]{1,0:T(8,128)S(1)}, u32[]{:S(2)}, u32[]{:S(2)}) collective-permute-start(f32[632,256]{1,0:T(8,128)S(1)} %get-tuple-element.191.own_down), channel_id=1, source_target_pairs={{1,0},{2,1},{3,2},{4,3},{5,4},{6,5},{7,6},{8,7},{9,8},{10,9},{11,1... | collective-permute-start | bytes 1941512 | tf_op jit(solution)/shard_map/ppermute | solution.py:464
  15.3 15.8 %collective-permute-start.15 = (f32[64,128]{1,0:T(8,128)S(1)}, f32[64,128]{1,0:T(8,128)S(1)}, u32[]{:S(2)}, u32[]{:S(2)}) collective-permute-start(f32[64,128]{1,0:T(8,128)S(1)} %get-tuple-element.180), channel_id=1, source_target_pairs={{2,0},{3,1},{4,2},{5,3},{6,4},{7,5},{8,6},{9,7},{10,8},{11,9},{12,... | collective-permute-start | bytes 98312 | tf_op jit(solution)/shard_map/ppermute | solution.py:464
  17.7 14.0 %collective-permute-start.14 = (f32[64,128]{1,0:T(8,128)S(1)}, f32[64,128]{1,0:T(8,128)S(1)}, u32[]{:S(2)}, u32[]{:S(2)}) collective-permute-start(f32[64,128]{1,0:T(8,128)S(1)} %get-tuple-element.180), channel_id=1, source_target_pairs={{0,2},{1,3},{2,4},{3,5},{4,6},{5,7},{6,8},{7,9},{8,10},{9,11},{10,... | collective-permute-start | bytes 98312 | tf_op jit(solution)/shard_map/ppermute | solution.py:463
  25.3 6.4 %copy-start.8 = (f32[2,64,128]{2,1,0:T(8,128)S(1)}, f32[2,64,128]{2,1,0:T(8,128)}, u32[]{:S(2)}) copy-start(f32[2,64,128]{2,1,0:T(8,128)} %currents.1) | copy-start | bytes 196612
  25.3 6.4 %copy-start.9 = (f32[128]{0:T(128)S(1)}, f32[128]{0:T(128)}, u32[]{:S(2)}) copy-start(f32[128]{0:T(128)} %param.31) | copy-start | bytes 1540
  25.3 6.4 %copy-start.10 = (s32[256]{0:T(256)S(1)}, s32[256]{0:T(256)}, u32[]{:S(2)}) copy-start(s32[256]{0:T(256)} %param.19) | copy-start | bytes 3076
  25.3 6.4 %copy-start.11 = (s32[4,128]{1,0:T(4,128)S(1)}, s32[4,128]{1,0:T(4,128)}, u32[]{:S(2)}) copy-start(s32[4,128]{1,0:T(4,128)} %ocean_index.1) | copy-start | bytes 6148
  35.4 23.0 %collective-permute-start.8 = (f32[632,256]{1,0:T(8,128)S(1)}, f32[632,256]{1,0:T(8,128)S(1)}, u32[]{:S(2)}, u32[]{:S(2)}) collective-permute-start(f32[632,256]{1,0:T(8,128)S(1)} %get-tuple-element.146.own_up), channel_id=1, source_target_pairs={{0,1},{1,2},{2,3},{3,4},{4,5},{5,6},{6,7},{7,8},{8,9},{9,10},{10,1... | collective-permute-start | bytes 1941512 | tf_op jit(solution)/shard_map/cond/branch_1_fun/ppermute | solution.py:463
  35.5 22.9 %collective-permute-start.9 = (f32[632,256]{1,0:T(8,128)S(1)}, f32[632,256]{1,0:T(8,128)S(1)}, u32[]{:S(2)}, u32[]{:S(2)}) collective-permute-start(f32[632,256]{1,0:T(8,128)S(1)} %get-tuple-element.147.own_down), channel_id=1, source_target_pairs={{1,0},{2,1},{3,2},{4,3},{5,4},{6,5},{7,6},{8,7},{9,8},{10,9},{11,1... | collective-permute-start | bytes 1941512 | tf_op jit(solution)/shard_map/cond/branch_1_fun/ppermute | solution.py:464
  42.7 15.7 %collective-permute-start.10 = (f32[8,256]{1,0:T(8,128)S(1)}, f32[8,256]{1,0:T(8,128)S(1)}, u32[]{:S(2)}, u32[]{:S(2)}) collective-permute-start(f32[8,256]{1,0:T(8,128)S(1)} %get-tuple-element.148), channel_id=1, source_target_pairs={{0,2},{1,3},{2,4},{3,5},{4,6},{5,7},{6,8},{7,9},{8,10},{9,11},{10,... | collective-permute-start | bytes 24584 | tf_op jit(solution)/shard_map/cond/branch_1_fun/ppermute | solution.py:463
  42.7 15.7 %collective-permute-start.11 = (f32[8,256]{1,0:T(8,128)S(1)}, f32[8,256]{1,0:T(8,128)S(1)}, u32[]{:S(2)}, u32[]{:S(2)}) collective-permute-start(f32[8,256]{1,0:T(8,128)S(1)} %get-tuple-element.149), channel_id=1, source_target_pairs={{2,0},{3,1},{4,2},{5,3},{6,4},{7,5},{8,6},{9,7},{10,8},{11,9},{12,... | collective-permute-start | bytes 24584 | tf_op jit(solution)/shard_map/cond/branch_1_fun/ppermute | solution.py:464
  61.8 10.1 %collective-permute-start.12 = (f32[192,128]{1,0:T(8,128)S(1)}, f32[192,128]{1,0:T(8,128)S(1)}, u32[]{:S(2)}, u32[]{:S(2)}) collective-permute-start(f32[192,128]{1,0:T(8,128)S(1)} %get-tuple-element.157), channel_id=1, source_target_pairs={{0,1},{1,2},{2,3},{3,4},{4,5},{5,6},{6,7},{7,8},{8,9},{9,10},{10,1... | collective-permute-start | bytes 294920 | tf_op jit(solution)/shard_map/cond/branch_1_fun/ppermute | solution.py:463
  61.9 10.0 %collective-permute-start.13 = (f32[192,128]{1,0:T(8,128)S(1)}, f32[192,128]{1,0:T(8,128)S(1)}, u32[]{:S(2)}, u32[]{:S(2)}) collective-permute-start(f32[192,128]{1,0:T(8,128)S(1)} %get-tuple-element.158), channel_id=1, source_target_pairs={{1,0},{2,1},{3,2},{4,3},{5,4},{6,5},{7,6},{8,7},{9,8},{10,9},{11,1... | collective-permute-start | bytes 294920 | tf_op jit(solution)/shard_map/cond/branch_1_fun/ppermute | solution.py:464
  (2 other events, 12.8 us)

commit v4 on v3

--- a/solution.py
+++ b/solution.py
@@ -110,7 +110,7 @@
 def table_kernel(
     row, pos, sign, courant, nonlinear, quad_index, quad_weight, stokes_table, point_index,
     point_weight, mixing, level, quad, back, stokes_sorted, wide, cell_column, cell_side, cell_weight,
-    mixing_wide, level_wide, select, rows, parts, columns,
+    mixing_wide, level_wide, origin, select, rows, parts, columns,
 ):
     one_hot_rows(select, pos)
     sense = (2 * sign[...] - 1).astype(F32)
@@ -169,6 +169,7 @@
             cell_column[line, :] = cell % OX
             cell_side[line, :] = (cell // OX - row[0] + 257) % 256
             cell_weight[line, :] = point_weight[config : config + 1, half * 128 : (half + 1) * 128]
+    origin[...] = jnp.zeros((1, OX), F32) + (row[0] * MX).astype(F32)
     diagonal = lax.broadcasted_iota(jnp.int32, (L, L), 0) == lax.broadcasted_iota(jnp.int32, (L, L), 1)
     for line, wide_column in ((mixing, mixing_wide), (level, level_wide)):
         column = jnp.sum(jnp.where(diagonal, line[...], 0.0), axis=1, keepdims=True)
@@ -176,7 +177,7 @@
 
 
 def cell_table(base, index, weight):
-    point = (lax.broadcasted_iota(jnp.int32, (MX, OX), 0) + base).astype(F32)
+    point = lax.broadcasted_iota(jnp.int32, (MX, OX), 0).astype(F32) + base
     total = jnp.zeros((MX, OX), F32)
     for config in range(4):
         total = total + jnp.where(
@@ -317,12 +318,12 @@
 
 
 def first_kernel(
-    count, row, own_up, own_down, from_below, from_above, below_two, above_two, surface, slope, quad, wide,
+    count, origin, own_up, own_down, from_below, from_above, below_two, above_two, surface, slope, quad, wide,
     stokes_sorted, cell_column, cell_side, cell_weight, wet, ocean_index, ocean_weight, currents,
     coriolis, mixing, level,
     up, down, own_part, surface_part, far_up, far_down, cells, cells_low, advected, rounded, finished,
 ):
-    base = row[0] * MX
+    base = origin[...]
     half = L // 2
     below_extra = from_below[count:, :]
     above_extra = from_above[count:, :]
@@ -491,7 +492,7 @@
         (
             shape(4, K, K, dtype=BF16), shape(K, K, dtype=BF16), shape(128, K, dtype=BF16),
             shape(7, K, 128), shape(8, OX, dtype=whole), shape(8, OX, dtype=whole), shape(8, OX),
-            shape(L, OX), shape(L, OX),
+            shape(L, OX), shape(L, OX), shape(1, OX),
         ),
         (pltpu.VMEM((K, K), BF16), pltpu.VMEM((32, K), F32), pltpu.VMEM((96, K), BF16),
          pltpu.VMEM((K, 32), F32)),
@@ -501,10 +502,10 @@
 
 
 def steps(
-    count, up, down, below, above, slope, below_two, above_two, surface, made, row, wet, ocean_index,
+    count, up, down, below, above, slope, below_two, above_two, surface, made, wet, ocean_index,
     ocean_weight, currents, coriolis,
 ):
-    quad, back, stokes_sorted, wide, cell_column, cell_side, cell_weight, mixing, level = made
+    quad, back, stokes_sorted, wide, cell_column, cell_side, cell_weight, mixing, level, origin = made
     part = shape(128, OX)
     message = shape(count + EXTRA, MX)
     far = shape(8, MX)
@@ -514,8 +515,8 @@
         functools.partial(first_kernel, count),
         (message, message, part, far, far, far, table, table),
         (pltpu.VMEM((K, MX), F32),) + work,
-        scalars=1, inputs=22, flops=3 << 30, data=12 << 20, name="first",
-    )(row, up, down, below, above, below_two, above_two, surface, slope, quad, wide, stokes_sorted,
+        inputs=22, flops=3 << 30, data=12 << 20, name="first",
+    )(origin, up, down, below, above, below_two, above_two, surface, slope, quad, wide, stokes_sorted,
       cell_column, cell_side, cell_weight, wet, ocean_index, ocean_weight, currents, coriolis, mixing,
       level)
     next_below, next_above = exchange(next_up, next_down)
@@ -561,7 +562,7 @@
     )
     slope = slopes(FAST, up, down, made[3])
     rest = (
-        below_two, above_two, surface, made, row, water_mask.reshape(1, MX), ocean_index, ocean_weight,
+        below_two, above_two, surface, made, water_mask.reshape(1, MX), ocean_index, ocean_weight,
         currents, rotation,
     )
 

time: 72.7 us -> 72.7 us (level)
  no operation moved by 1% of the time
where the time goes in v4:
time: 72.7 us; the launch traced here: 72.6 us
  starting transfers between devices  36.8 us (51%)
  Pallas kernels  21.2 us (29%)
  waiting for transfers between devices  12.7 us (17%)
  between operations  1.54 us (2%)
    ppermute x5, starting transfers between devices, exchange(): lax.ppermute(to_below, AXES, [(b, a) for a, b in up])  34 us
    ppermute x5, waiting for transfers between devices, exchange(): lax.ppermute(to_above, AXES, up)  8.27 us
    pallas_call x1, Pallas kernels, tables(): call(table_kernel, (shape(4, K, K, dtype=BF16), shape(K, K, dtype=BF16),...  7.5 us
    ppermute x5, waiting for transfers between devices, exchange(): lax.ppermute(to_below, AXES, [(b, a) for a, b in up])  4.45 us
    pallas_call x1, Pallas kernels, steps(): call(functools.partial(first_kernel, count), (message, message, part, far...  3.41 us
    pallas_call x1, Pallas kernels, steps(): call(functools.partial(second_kernel, count), (shape(K, MX), shape(2, L,...  3.35 us
    pallas_call x1, Pallas kernels, pack(): call(functools.partial(pack_kernel, count), (message, message, shape(8, 1...  2.8 us
    ppermute x5, starting transfers between devices, exchange(): lax.ppermute(to_above, AXES, up)  2.74 us
  transfers between devices with their start and end apart: 10, of which 4 were waited for; matrix products, arithmetic and copies ran while one was open for 0% of the time, Pallas kernels for 15%

profile of v4, /device:TPU:1, one launch (start us, length us, event | category | flops | bytes accessed | tf_op | source)
XLA Modules:
  0.0 72.6 jit_solution(9212138039043612303)
XLA Ops:
  0.7 2.8 %pack.3 = (f32[632,256]{1,0:T(8,128)S(1)}, f32[632,256]{1,0:T(8,128)S(1)}, f32[8,128]{1,0:T(8,128)S(1)}, f32[8,128]{1,0:T(8,128)S(1)}, f32[64,128]{1,0:T(8,128)S(1)}, /*index=5*/s32[1]{0:T(128)}) custom-call(s32[2,1024]{1,0:T(2,128)} %sign.3, f32[1024,256]{1,0:T(8,128)} %spectrum.1, f32[2,64,128]{2,1,0:T(8,128)} %currents.1, f32[1,64]{1,0:T(1,128)} %bitcast.18, ...), custom_call_target="tpu_custom_call" | custom-call | flops 1610612736 | bytes 1048576 | tf_op jit(solution)/shard_map/pack/pallas_call | solution.py:471
  3.5 2.5 %collective-permute-start.16 = (f32[632,256]{1,0:T(8,128)S(1)}, f32[632,256]{1,0:T(8,128)S(1)}, u32[]{:S(2)}, u32[]{:S(2)}) collective-permute-start(f32[632,256]{1,0:T(8,128)S(1)} %get-tuple-element.192.own_up), channel_id=1, source_target_pairs={{0,1},{1,2},{2,3},{3,4},{4,5},{5,6},{6,7},{7,8},{8,9},{9,10},{10,1... | collective-permute-start | bytes 1941512 | tf_op jit(solution)/shard_map/ppermute | solution.py:464
  6.1 9.2 %collective-permute-start.17 = (f32[632,256]{1,0:T(8,128)S(1)}, f32[632,256]{1,0:T(8,128)S(1)}, u32[]{:S(2)}, u32[]{:S(2)}) collective-permute-start(f32[632,256]{1,0:T(8,128)S(1)} %get-tuple-element.193.own_down), channel_id=1, source_target_pairs={{1,0},{2,1},{3,2},{4,3},{5,4},{6,5},{7,6},{8,7},{9,8},{10,9},{11,1... | collective-permute-start | bytes 1941512 | tf_op jit(solution)/shard_map/ppermute | solution.py:465
  15.3 2.4 %collective-permute-start.15 = (f32[64,128]{1,0:T(8,128)S(1)}, f32[64,128]{1,0:T(8,128)S(1)}, u32[]{:S(2)}, u32[]{:S(2)}) collective-permute-start(f32[64,128]{1,0:T(8,128)S(1)} %get-tuple-element.182), channel_id=1, source_target_pairs={{2,0},{3,1},{4,2},{5,3},{6,4},{7,5},{8,6},{9,7},{10,8},{11,9},{12,... | collective-permute-start | bytes 98312 | tf_op jit(solution)/shard_map/ppermute | solution.py:465
  17.7 0.0 collective-permute-start.14
  17.8 7.5 %tables.1 = (bf16[4,1024,1024]{2,1,0:T(8,128)(2,1)S(1)}, bf16[1024,1024]{1,0:T(8,128)(2,1)S(1)}, bf16[128,1024]{1,0:T(8,128)(2,1)S(1)}, f32[7,1024,128]{2,1,0:T(...) custom-call(s32[1]{0:T(128)} %bitcast.3.row, ...), custom_call_target="tpu_custom_call" | custom-call | flops 4294967296 | bytes 12582912 | tf_op jit(solution)/shard_map/tables/pallas_call | solution.py:490
  25.3 0.0 copy-start.9
  25.3 0.0 copy-start.10
  25.4 0.6 slopes.7
  26.7 4.4 %collective-permute-done.15 = f32[64,128]{1,0:T(8,128)S(1)} collective-permute-done((f32[64,128]{1,0:T(8,128)S(1)}, f32[64,128]{1,0:T(8,128)S(1)}, u32[]{:S(2)}, u32[]{:S(2)}) %collective-permute-start.15) | collective-permute-done | bytes 32800 | tf_op jit(solution)/shard_map/ppermute | solution.py:465
  31.1 0.6 collective-permute-done.14
  31.8 40.8 %conditional.1 = (f32[1024,256]{1,0:T(8,128)}, f32[2,64,128]{2,1,0:T(8,128)}) conditional(s32[]{:T(128)} %bitcast.2, (s32[2,1024]{1,0:T(2,128)S(1)}, f32[1024,256]{1,0:T(8,128)S(1)}, f32[2,64,128]{2,1,0:T(8,128)S(1)}, f32[1,64]{1,0:T(1,128)S(1)}, f32[1,128]{1,0:T(1,128)S(1)}, /*index=5*/s32[4,128]{1,0:T(4,128)S(1)}, f32[4,128]{1,0:T(4,128)S(1)}, ...), branch_computations={%region_0.0_spmd, %region_1.0_spmd} | conditional | flops 11275337728 | bytes 57868624 | solution.py:577
  32.0 3.4 %first.3 = (f32[632,256]{1,0:T(8,128)S(1)}, f32[632,256]{1,0:T(8,128)S(1)}, f32[128,128]{1,0:T(8,128)S(1)}, f32[8,256]{1,0:T(8,128)S(1)}, f32[8,256]{1,0:T(8,128...) custom-call(f32[1,128]{1,0:T(1,128)S(1)} %get-tuple-element.124.origin, ...), custom_call_target="tpu_custom_call" | custom-call | flops 3221225472 | bytes 12582912 | tf_op jit(solution)/shard_map/cond/branch_1_fun/first/pallas_call | solution.py:514
  35.4 0.1 collective-permute-start.8
  35.5 7.2 %collective-permute-start.9 = (f32[632,256]{1,0:T(8,128)S(1)}, f32[632,256]{1,0:T(8,128)S(1)}, u32[]{:S(2)}, u32[]{:S(2)}) collective-permute-start(f32[632,256]{1,0:T(8,128)S(1)} %get-tuple-element.147.own_down), channel_id=1, source_target_pairs={{1,0},{2,1},{3,2},{4,3},{5,4},{6,5},{7,6},{8,7},{9,8},{10,9},{11,1... | collective-permute-start | bytes 1941512 | tf_op jit(solution)/shard_map/cond/branch_1_fun/ppermute | solution.py:465
  42.7 8.1 %collective-permute-start.11 = (f32[8,256]{1,0:T(8,128)S(1)}, f32[8,256]{1,0:T(8,128)S(1)}, u32[]{:S(2)}, u32[]{:S(2)}) collective-permute-start(f32[8,256]{1,0:T(8,128)S(1)} %get-tuple-element.149), channel_id=1, source_target_pairs={{2,0},{3,1},{4,2},{5,3},{6,4},{7,5},{8,6},{9,7},{10,8},{11,9},{12,... | collective-permute-start | bytes 24584 | tf_op jit(solution)/shard_map/cond/branch_1_fun/ppermute | solution.py:465
  50.8 0.6 slopes.6.slope
  51.4 7.0 %collective-permute-done.10.below_two = f32[8,256]{1,0:T(8,128)S(1)} collective-permute-done((f32[8,256]{1,0:T(8,128)S(1)}, f32[8,256]{1,0:T(8,128)S(1)}, u32[]{:S(2)}, u32[]{:S(2)}) %collective-permute-start.10) | collective-permute-done | bytes 8224 | tf_op jit(solution)/shard_map/cond/branch_1_fun/ppermute | solution.py:464
  58.4 3.3 %second.3 = (f32[1024,256]{1,0:T(8,128)S(1)}, f32[2,64,128]{2,1,0:T(8,128)S(1)}, f32[192,128]{1,0:T(8,128)S(1)}, f32[192,128]{1,0:T(8,128)S(1)}, f32[128,128]{1,0:T(8,128)S(1)}) custom-call(f32[632,256]{1,0:T(8,128)S(1)} %get-tuple-element.146.own_up, f32[632,256]{1,0:T(8,128)S(1)} %get-tuple-element.147.own_down, ...), custom_call_target="tpu_custom_call" | custom-call | flops 3221225472 | bytes 12582912 | tf_op jit(solution)/shard_map/cond/branch_1_fun/second/pallas_call | solution.py:526
  61.8 0.1 collective-permute-start.12
  61.9 7.2 %collective-permute-start.13 = (f32[192,128]{1,0:T(8,128)S(1)}, f32[192,128]{1,0:T(8,128)S(1)}, u32[]{:S(2)}, u32[]{:S(2)}) collective-permute-start(f32[192,128]{1,0:T(8,128)S(1)} %get-tuple-element.158), channel_id=1, source_target_pairs={{1,0},{2,1},{3,2},{4,3},{5,4},{6,5},{7,6},{8,7},{9,8},{10,9},{11,1... | collective-permute-start | bytes 294920 | tf_op jit(solution)/shard_map/cond/branch_1_fun/ppermute | solution.py:465
  69.0 2.2 %restore.3 = f32[1024,256]{1,0:T(8,128)} custom-call(f32[1024,256]{1,0:T(8,128)S(1)} %get-tuple-element.154.spectra, bf16[1024,1024]{1,0:T(8,128)(2,1)S(1)} %get-tuple-element.155.back), custom_call_target="tpu_custom_call" | custom-call | flops 1073741824 | bytes 4194304 | tf_op jit(solution)/shard_map/cond/branch_1_fun/restore/pallas_call | solution.py:534
  71.3 0.6 collective-permute-done.12.from_below
  71.9 0.7 ocean.3
  (37 shorter events, 0.1 us)
Async XLA Ops:
  0.6 17.1 %copy-start = (bf16[128,1024]{1,0:T(8,128)(2,1)S(1)}, bf16[128,1024]{1,0:T(8,128)(2,1)}, u32[]{:S(2)}) copy-start(bf16[128,1024]{1,0:T(8,128)(2,1)} %stokes_table.1) | copy-start | bytes 786436
  0.6 17.1 %copy-start.1 = (s32[4,1024,2]{1,2,0:T(2,128)S(1)}, s32[4,1024,2]{1,2,0:T(2,128)}, u32[]{:S(2)}) copy-start(s32[4,1024,2]{1,2,0:T(2,128)} %param.22) | copy-start | bytes 98308
  0.7 17.1 %copy-start.2 = (f32[4,1024,2]{1,2,0:T(2,128)S(1)}, f32[4,1024,2]{1,2,0:T(2,128)}, u32[]{:S(2)}) copy-start(f32[4,1024,2]{1,2,0:T(2,128)} %param.23) | copy-start | bytes 98308
  0.7 17.1 %copy-start.3 = (f32[2,1024]{1,0:T(2,128)S(1)}, f32[2,1024]{1,0:T(2,128)}, u32[]{:S(2)}) copy-start(f32[2,1024]{1,0:T(2,128)} %courant.1) | copy-start | bytes 24580
  0.7 17.1 %copy-start.4 = (f32[1024]{0:T(1024)S(1)}, f32[1024]{0:T(1024)}, u32[]{:S(2)}) copy-start(f32[1024]{0:T(1024)} %param.24) | copy-start | bytes 12292
  0.7 17.1 %copy-start.5 = (s32[4,256]{1,0:T(4,128)S(1)}, s32[4,256]{1,0:T(4,128)}, u32[]{:S(2)}) copy-start(s32[4,256]{1,0:T(4,128)} %point_index.1) | copy-start | bytes 12292
  0.7 17.1 %copy-start.6 = (f32[4,256]{1,0:T(4,128)S(1)}, f32[4,256]{1,0:T(4,128)}, u32[]{:S(2)}) copy-start(f32[4,256]{1,0:T(4,128)} %point_weight.1) | copy-start | bytes 12292
  0.7 17.1 %copy-start.7 = (f32[64]{0:T(128)S(1)}, f32[64]{0:T(128)}, u32[]{:S(2)}) copy-start(f32[64]{0:T(128)} %param.32) | copy-start | bytes 772
  0.7 17.1 %copy-start.14 = (s32[2,1024]{1,0:T(2,128)S(1)}, s32[2,1024]{1,0:T(2,128)}, u32[]{:S(2)}) copy-start(s32[2,1024]{1,0:T(2,128)} %sign.3) | copy-start | bytes 24580
  0.7 17.1 %copy-start.15 = (f32[64]{0:T(128)S(1)}, f32[64]{0:T(128)}, u32[]{:S(2)}) copy-start(f32[64]{0:T(128)} %param.33) | copy-start | bytes 772
  3.5 28.2 %collective-permute-start.16 = (f32[632,256]{1,0:T(8,128)S(1)}, f32[632,256]{1,0:T(8,128)S(1)}, u32[]{:S(2)}, u32[]{:S(2)}) collective-permute-start(f32[632,256]{1,0:T(8,128)S(1)} %get-tuple-element.192.own_up), channel_id=1, source_target_pairs={{0,1},{1,2},{2,3},{3,4},{4,5},{5,6},{6,7},{7,8},{8,9},{9,10},{10,1... | collective-permute-start | bytes 1941512 | tf_op jit(solution)/shard_map/ppermute | solution.py:464
  6.1 25.6 %collective-permute-start.17 = (f32[632,256]{1,0:T(8,128)S(1)}, f32[632,256]{1,0:T(8,128)S(1)}, u32[]{:S(2)}, u32[]{:S(2)}) collective-permute-start(f32[632,256]{1,0:T(8,128)S(1)} %get-tuple-element.193.own_down), channel_id=1, source_target_pairs={{1,0},{2,1},{3,2},{4,3},{5,4},{6,5},{7,6},{8,7},{9,8},{10,9},{11,1... | collective-permute-start | bytes 1941512 | tf_op jit(solution)/shard_map/ppermute | solution.py:465
  15.3 15.8 %collective-permute-start.15 = (f32[64,128]{1,0:T(8,128)S(1)}, f32[64,128]{1,0:T(8,128)S(1)}, u32[]{:S(2)}, u32[]{:S(2)}) collective-permute-start(f32[64,128]{1,0:T(8,128)S(1)} %get-tuple-element.182), channel_id=1, source_target_pairs={{2,0},{3,1},{4,2},{5,3},{6,4},{7,5},{8,6},{9,7},{10,8},{11,9},{12,... | collective-permute-start | bytes 98312 | tf_op jit(solution)/shard_map/ppermute | solution.py:465
  17.7 14.0 %collective-permute-start.14 = (f32[64,128]{1,0:T(8,128)S(1)}, f32[64,128]{1,0:T(8,128)S(1)}, u32[]{:S(2)}, u32[]{:S(2)}) collective-permute-start(f32[64,128]{1,0:T(8,128)S(1)} %get-tuple-element.182), channel_id=1, source_target_pairs={{0,2},{1,3},{2,4},{3,5},{4,6},{5,7},{6,8},{7,9},{8,10},{9,11},{10,... | collective-permute-start | bytes 98312 | tf_op jit(solution)/shard_map/ppermute | solution.py:464
  25.3 6.4 %copy-start.8 = (f32[2,64,128]{2,1,0:T(8,128)S(1)}, f32[2,64,128]{2,1,0:T(8,128)}, u32[]{:S(2)}) copy-start(f32[2,64,128]{2,1,0:T(8,128)} %currents.1) | copy-start | bytes 196612
  25.3 6.4 %copy-start.9 = (f32[128]{0:T(128)S(1)}, f32[128]{0:T(128)}, u32[]{:S(2)}) copy-start(f32[128]{0:T(128)} %param.31) | copy-start | bytes 1540
  25.3 6.4 %copy-start.10 = (s32[256]{0:T(256)S(1)}, s32[256]{0:T(256)}, u32[]{:S(2)}) copy-start(s32[256]{0:T(256)} %param.19) | copy-start | bytes 3076
  25.3 6.4 %copy-start.11 = (s32[4,128]{1,0:T(4,128)S(1)}, s32[4,128]{1,0:T(4,128)}, u32[]{:S(2)}) copy-start(s32[4,128]{1,0:T(4,128)} %ocean_index.1) | copy-start | bytes 6148
  35.4 23.0 %collective-permute-start.8 = (f32[632,256]{1,0:T(8,128)S(1)}, f32[632,256]{1,0:T(8,128)S(1)}, u32[]{:S(2)}, u32[]{:S(2)}) collective-permute-start(f32[632,256]{1,0:T(8,128)S(1)} %get-tuple-element.146.own_up), channel_id=1, source_target_pairs={{0,1},{1,2},{2,3},{3,4},{4,5},{5,6},{6,7},{7,8},{8,9},{9,10},{10,1... | collective-permute-start | bytes 1941512 | tf_op jit(solution)/shard_map/cond/branch_1_fun/ppermute | solution.py:464
  35.5 22.9 %collective-permute-start.9 = (f32[632,256]{1,0:T(8,128)S(1)}, f32[632,256]{1,0:T(8,128)S(1)}, u32[]{:S(2)}, u32[]{:S(2)}) collective-permute-start(f32[632,256]{1,0:T(8,128)S(1)} %get-tuple-element.147.own_down), channel_id=1, source_target_pairs={{1,0},{2,1},{3,2},{4,3},{5,4},{6,5},{7,6},{8,7},{9,8},{10,9},{11,1... | collective-permute-start | bytes 1941512 | tf_op jit(solution)/shard_map/cond/branch_1_fun/ppermute | solution.py:465
  42.7 15.7 %collective-permute-start.10 = (f32[8,256]{1,0:T(8,128)S(1)}, f32[8,256]{1,0:T(8,128)S(1)}, u32[]{:S(2)}, u32[]{:S(2)}) collective-permute-start(f32[8,256]{1,0:T(8,128)S(1)} %get-tuple-element.148), channel_id=1, source_target_pairs={{0,2},{1,3},{2,4},{3,5},{4,6},{5,7},{6,8},{7,9},{8,10},{9,11},{10,... | collective-permute-start | bytes 24584 | tf_op jit(solution)/shard_map/cond/branch_1_fun/ppermute | solution.py:464
  42.7 15.7 %collective-permute-start.11 = (f32[8,256]{1,0:T(8,128)S(1)}, f32[8,256]{1,0:T(8,128)S(1)}, u32[]{:S(2)}, u32[]{:S(2)}) collective-permute-start(f32[8,256]{1,0:T(8,128)S(1)} %get-tuple-element.149), channel_id=1, source_target_pairs={{2,0},{3,1},{4,2},{5,3},{6,4},{7,5},{8,6},{9,7},{10,8},{11,9},{12,... | collective-permute-start | bytes 24584 | tf_op jit(solution)/shard_map/cond/branch_1_fun/ppermute | solution.py:465
  61.8 10.1 %collective-permute-start.12 = (f32[192,128]{1,0:T(8,128)S(1)}, f32[192,128]{1,0:T(8,128)S(1)}, u32[]{:S(2)}, u32[]{:S(2)}) collective-permute-start(f32[192,128]{1,0:T(8,128)S(1)} %get-tuple-element.157), channel_id=1, source_target_pairs={{0,1},{1,2},{2,3},{3,4},{4,5},{5,6},{6,7},{7,8},{8,9},{9,10},{10,1... | collective-permute-start | bytes 294920 | tf_op jit(solution)/shard_map/cond/branch_1_fun/ppermute | solution.py:464
  61.9 10.0 %collective-permute-start.13 = (f32[192,128]{1,0:T(8,128)S(1)}, f32[192,128]{1,0:T(8,128)S(1)}, u32[]{:S(2)}, u32[]{:S(2)}) collective-permute-start(f32[192,128]{1,0:T(8,128)S(1)} %get-tuple-element.158), channel_id=1, source_target_pairs={{1,0},{2,1},{3,2},{4,3},{5,4},{6,5},{7,6},{8,7},{9,8},{10,9},{11,1... | collective-permute-start | bytes 294920 | tf_op jit(solution)/shard_map/cond/branch_1_fun/ppermute | solution.py:465
  (2 other events, 12.8 us)

commit v5 on v3

--- a/solution.py
+++ b/solution.py
@@ -109,8 +109,8 @@
 
 def table_kernel(
     row, pos, sign, courant, nonlinear, quad_index, quad_weight, stokes_table, point_index,
-    point_weight, mixing, level, quad, back, stokes_sorted, wide, cell_column, cell_side, cell_weight,
-    mixing_wide, level_wide, select, rows, parts, columns,
+    point_weight, mixing, level, ocean_index, ocean_weight, quad, back, stokes_sorted, wide, cell_column, cell_side, cell_weight,
+    mixing_wide, level_wide, own_cells, own_low, select, rows, parts, columns,
 ):
     one_hot_rows(select, pos)
     sense = (2 * sign[...] - 1).astype(F32)
@@ -169,6 +169,8 @@
             cell_column[line, :] = cell % OX
             cell_side[line, :] = (cell // OX - row[0] + 257) % 256
             cell_weight[line, :] = point_weight[config : config + 1, half * 128 : (half + 1) * 128]
+    table = cell_table(row[0] * MX, ocean_index[...].astype(F32), ocean_weight[...])
+    own_cells[...], own_low[...] = split2(table)
     diagonal = lax.broadcasted_iota(jnp.int32, (L, L), 0) == lax.broadcasted_iota(jnp.int32, (L, L), 1)
     for line, wide_column in ((mixing, mixing_wide), (level, level_wide)):
         column = jnp.sum(jnp.where(diagonal, line[...], 0.0), axis=1, keepdims=True)
@@ -318,7 +320,7 @@
 
 def first_kernel(
     count, row, own_up, own_down, from_below, from_above, below_two, above_two, surface, slope, quad, wide,
-    stokes_sorted, cell_column, cell_side, cell_weight, wet, ocean_index, ocean_weight, currents,
+    stokes_sorted, cell_column, cell_side, cell_weight, wet, own_cells, own_low, currents,
     coriolis, mixing, level,
     up, down, own_part, surface_part, far_up, far_down, cells, cells_low, advected, rounded, finished,
 ):
@@ -328,13 +330,14 @@
     above_extra = from_above[count:, :]
     for side, index, weight in (
         (0, below_extra[1:5, 0:OX], below_extra[1:5, OX:]),
-        (1, ocean_index[...].astype(F32), ocean_weight[...]),
         (2, above_extra[1:5, 0:OX], above_extra[1:5, OX:]),
     ):
         table = cell_table(base, index, weight)
         high = table.astype(BF16)
         cells[:, side * OX : (side + 1) * OX] = high
         cells_low[:, side * OX : (side + 1) * OX] = (table - high.astype(F32)).astype(BF16)
+    cells[:, OX : 2 * OX] = own_cells[...]
+    cells_low[:, OX : 2 * OX] = own_low[...]
     own = jnp.concatenate([surface[0:1, :], surface[1:2, :]], axis=1)
     sides = (below_extra[0:1, :], own, above_extra[0:1, :])
     flow = flow_of(sides, cell_column, cell_side, cell_weight)
@@ -484,27 +487,27 @@
 
 
 def tables(row, pos, stencil_sign, courant, nonlinear, quad_index, quad_weight, stokes_table, point_index,
-           point_weight, mixing, level):
+           point_weight, mixing, level, ocean_index, ocean_weight):
     whole = jnp.int32
     return call(
         table_kernel,
         (
             shape(4, K, K, dtype=BF16), shape(K, K, dtype=BF16), shape(128, K, dtype=BF16),
             shape(7, K, 128), shape(8, OX, dtype=whole), shape(8, OX, dtype=whole), shape(8, OX),
-            shape(L, OX), shape(L, OX),
+            shape(L, OX), shape(L, OX), shape(MX, OX, dtype=BF16), shape(MX, OX, dtype=BF16),
         ),
         (pltpu.VMEM((K, K), BF16), pltpu.VMEM((32, K), F32), pltpu.VMEM((96, K), BF16),
          pltpu.VMEM((K, 32), F32)),
-        scalars=1, inputs=12, flops=4 << 30, data=12 << 20, name="tables",
+        scalars=1, inputs=14, flops=4 << 30, data=12 << 20, name="tables",
     )(row, pos, stencil_sign, courant, nonlinear, quad_index, quad_weight, stokes_table, point_index,
-      point_weight, mixing, level)
+      point_weight, mixing, level, ocean_index, ocean_weight)
 
 
 def steps(
-    count, up, down, below, above, slope, below_two, above_two, surface, made, row, wet, ocean_index,
-    ocean_weight, currents, coriolis,
+    count, up, down, below, above, slope, below_two, above_two, surface, made, row, wet,
+    currents, coriolis,
 ):
-    quad, back, stokes_sorted, wide, cell_column, cell_side, cell_weight, mixing, level = made
+    quad, back, stokes_sorted, wide, cell_column, cell_side, cell_weight, mixing, level, own_cells, own_low = made
     part = shape(128, OX)
     message = shape(count + EXTRA, MX)
     far = shape(8, MX)
@@ -516,7 +519,7 @@
         (pltpu.VMEM((K, MX), F32),) + work,
         scalars=1, inputs=22, flops=3 << 30, data=12 << 20, name="first",
     )(row, up, down, below, above, below_two, above_two, surface, slope, quad, wide, stokes_sorted,
-      cell_column, cell_side, cell_weight, wet, ocean_index, ocean_weight, currents, coriolis, mixing,
+      cell_column, cell_side, cell_weight, wet, own_cells, own_low, currents, coriolis, mixing,
       level)
     next_below, next_above = exchange(next_up, next_down)
     far_below, far_above = exchange(far_up, far_down, 2)
@@ -557,11 +560,11 @@
     made = tables(
         row, pos, stencil_sign, courant, nonlinear.reshape(1, K), quad_index.transpose(0, 2, 1),
         quad_weight.transpose(0, 2, 1), stokes_table, point_index, point_weight, mixing.reshape(1, L),
-        level,
+        level, ocean_index, ocean_weight,
     )
     slope = slopes(FAST, up, down, made[3])
     rest = (
-        below_two, above_two, surface, made, row, water_mask.reshape(1, MX), ocean_index, ocean_weight,
+        below_two, above_two, surface, made, row, water_mask.reshape(1, MX),
         currents, rotation,
     )
 

time: 72.7 us -> 72.7 us (level)
  no operation moved by 1% of the time
where the time goes in v5:
time: 72.7 us; the launch traced here: 72.5 us
  starting transfers between devices  36.8 us (51%)
  Pallas kernels  21.2 us (29%)
  waiting for transfers between devices  12.7 us (17%)
  between operations  1.54 us (2%)
    ppermute x5, starting transfers between devices, exchange(): lax.ppermute(to_below, AXES, [(b, a) for a, b in up])  34 us
    ppermute x5, waiting for transfers between devices, exchange(): lax.ppermute(to_above, AXES, up)  8.28 us
    pallas_call x1, Pallas kernels, tables(): call(table_kernel, (shape(4, K, K, dtype=BF16), shape(K, K, dtype=BF16),...  7.54 us
    ppermute x5, waiting for transfers between devices, exchange(): lax.ppermute(to_below, AXES, [(b, a) for a, b in up])  4.42 us
    pallas_call x1, Pallas kernels, steps(): call(functools.partial(first_kernel, count), (message, message, part, far...  3.36 us
    pallas_call x1, Pallas kernels, steps(): call(functools.partial(second_kernel, count), (shape(K, MX), shape(2, L,...  3.33 us
    pallas_call x1, Pallas kernels, pack(): call(functools.partial(pack_kernel, count), (message, message, shape(8, 1...  2.79 us
    ppermute x5, starting transfers between devices, exchange(): lax.ppermute(to_above, AXES, up)  2.74 us
  transfers between devices with their start and end apart: 10, of which 4 were waited for; matrix products, arithmetic and copies ran while one was open for 0% of the time, Pallas kernels for 15%

profile of v5, /device:TPU:1, one launch (start us, length us, event | category | flops | bytes accessed | tf_op | source)
XLA Modules:
  0.0 72.5 jit_solution(13921308735297495160)
XLA Ops:
  0.8 2.8 %pack.3 = (f32[632,256]{1,0:T(8,128)S(1)}, f32[632,256]{1,0:T(8,128)S(1)}, f32[8,128]{1,0:T(8,128)S(1)}, f32[8,128]{1,0:T(8,128)S(1)}, f32[64,128]{1,0:T(8,128)S(1)}, /*index=5*/s32[1]{0:T(128)}) custom-call(s32[2,1024]{1,0:T(2,128)} %sign.3, f32[1024,256]{1,0:T(8,128)} %spectrum.1, f32[2,64,128]{2,1,0:T(8,128)} %currents.1, f32[1,64]{1,0:T(1,128)} %bitcast.18, ...), custom_call_target="tpu_custom_call" | custom-call | flops 1610612736 | bytes 1048576 | tf_op jit(solution)/shard_map/pack/pallas_call | solution.py:473
  3.6 2.5 %collective-permute-start.16 = (f32[632,256]{1,0:T(8,128)S(1)}, f32[632,256]{1,0:T(8,128)S(1)}, u32[]{:S(2)}, u32[]{:S(2)}) collective-permute-start(f32[632,256]{1,0:T(8,128)S(1)} %get-tuple-element.200.own_up), channel_id=1, source_target_pairs={{0,1},{1,2},{2,3},{3,4},{4,5},{5,6},{6,7},{7,8},{8,9},{9,10},{10,1... | collective-permute-start | bytes 1941512 | tf_op jit(solution)/shard_map/ppermute | solution.py:466
  6.1 9.2 %collective-permute-start.17 = (f32[632,256]{1,0:T(8,128)S(1)}, f32[632,256]{1,0:T(8,128)S(1)}, u32[]{:S(2)}, u32[]{:S(2)}) collective-permute-start(f32[632,256]{1,0:T(8,128)S(1)} %get-tuple-element.201.own_down), channel_id=1, source_target_pairs={{1,0},{2,1},{3,2},{4,3},{5,4},{6,5},{7,6},{8,7},{9,8},{10,9},{11,1... | collective-permute-start | bytes 1941512 | tf_op jit(solution)/shard_map/ppermute | solution.py:467
  15.3 2.4 %collective-permute-start.15 = (f32[64,128]{1,0:T(8,128)S(1)}, f32[64,128]{1,0:T(8,128)S(1)}, u32[]{:S(2)}, u32[]{:S(2)}) collective-permute-start(f32[64,128]{1,0:T(8,128)S(1)} %get-tuple-element.188), channel_id=1, source_target_pairs={{2,0},{3,1},{4,2},{5,3},{6,4},{7,5},{8,6},{9,7},{10,8},{11,9},{12,... | collective-permute-start | bytes 98312 | tf_op jit(solution)/shard_map/ppermute | solution.py:467
  17.7 0.0 collective-permute-start.14
  17.8 7.5 %tables.1 = (bf16[4,1024,1024]{2,1,0:T(8,128)(2,1)S(1)}, bf16[1024,1024]{1,0:T(8,128)(2,1)S(1)}, bf16[128,1024]{1,0:T(8,128)(2,1)S(1)}, f32[7,1024,128]{2,1,0:T(...) custom-call(s32[1]{0:T(128)} %bitcast.3.row, ...), custom_call_target="tpu_custom_call" | custom-call | flops 4294967296 | bytes 12582912 | tf_op jit(solution)/shard_map/tables/pallas_call | solution.py:492
  25.4 0.0 copy-start.8
  25.4 0.0 copy-start.10
  25.4 0.6 slopes.7
  26.7 4.4 %collective-permute-done.15 = f32[64,128]{1,0:T(8,128)S(1)} collective-permute-done((f32[64,128]{1,0:T(8,128)S(1)}, f32[64,128]{1,0:T(8,128)S(1)}, u32[]{:S(2)}, u32[]{:S(2)}) %collective-permute-start.15) | collective-permute-done | bytes 32800 | tf_op jit(solution)/shard_map/ppermute | solution.py:467
  31.1 0.6 collective-permute-done.14
  31.8 40.8 %conditional.1 = (f32[1024,256]{1,0:T(8,128)}, f32[2,64,128]{2,1,0:T(8,128)}) conditional(s32[]{:T(128)} %bitcast.2, (s32[2,1024]{1,0:T(2,128)S(1)}, f32[1024,256]{1,0:T(8,128)S(1)}, f32[2,64,128]{2,1,0:T(8,128)S(1)}, f32[1,64]{1,0:T(1,128)S(1)}, f32[1,128]{1,0:T(1,128)S(1)}, /*index=5*/s32[4,128]{1,0:T(4,128)S(1)}, f32[4,128]{1,0:T(4,128)S(1)}, ...), branch_computations={%region_0.0_spmd, %region_1.0_spmd} | conditional | flops 11275337728 | bytes 57868624 | solution.py:579
  32.0 3.4 %first.3 = (f32[632,256]{1,0:T(8,128)S(1)}, f32[632,256]{1,0:T(8,128)S(1)}, f32[128,128]{1,0:T(8,128)S(1)}, f32[8,256]{1,0:T(8,128)S(1)}, f32[8,256]{1,0:T(8,128...) custom-call(s32[1]{0:T(128)} %get-tuple-element.130.row, ...), custom_call_target="tpu_custom_call" | custom-call | flops 3221225472 | bytes 12582912 | tf_op jit(solution)/shard_map/cond/branch_1_fun/first/pallas_call | solution.py:516
  35.4 0.1 collective-permute-start.8
  35.5 7.2 %collective-permute-start.9 = (f32[632,256]{1,0:T(8,128)S(1)}, f32[632,256]{1,0:T(8,128)S(1)}, u32[]{:S(2)}, u32[]{:S(2)}) collective-permute-start(f32[632,256]{1,0:T(8,128)S(1)} %get-tuple-element.153.own_down), channel_id=1, source_target_pairs={{1,0},{2,1},{3,2},{4,3},{5,4},{6,5},{7,6},{8,7},{9,8},{10,9},{11,1... | collective-permute-start | bytes 1941512 | tf_op jit(solution)/shard_map/cond/branch_1_fun/ppermute | solution.py:467
  42.6 8.1 %collective-permute-start.11 = (f32[8,256]{1,0:T(8,128)S(1)}, f32[8,256]{1,0:T(8,128)S(1)}, u32[]{:S(2)}, u32[]{:S(2)}) collective-permute-start(f32[8,256]{1,0:T(8,128)S(1)} %get-tuple-element.155), channel_id=1, source_target_pairs={{2,0},{3,1},{4,2},{5,3},{6,4},{7,5},{8,6},{9,7},{10,8},{11,9},{12,... | collective-permute-start | bytes 24584 | tf_op jit(solution)/shard_map/cond/branch_1_fun/ppermute | solution.py:467
  50.7 0.6 slopes.6.slope
  51.3 7.0 %collective-permute-done.10.below_two = f32[8,256]{1,0:T(8,128)S(1)} collective-permute-done((f32[8,256]{1,0:T(8,128)S(1)}, f32[8,256]{1,0:T(8,128)S(1)}, u32[]{:S(2)}, u32[]{:S(2)}) %collective-permute-start.10) | collective-permute-done | bytes 8224 | tf_op jit(solution)/shard_map/cond/branch_1_fun/ppermute | solution.py:466
  58.4 3.3 %second.3 = (f32[1024,256]{1,0:T(8,128)S(1)}, f32[2,64,128]{2,1,0:T(8,128)S(1)}, f32[192,128]{1,0:T(8,128)S(1)}, f32[192,128]{1,0:T(8,128)S(1)}, f32[128,128]{1,0:T(8,128)S(1)}) custom-call(f32[632,256]{1,0:T(8,128)S(1)} %get-tuple-element.152.own_up, f32[632,256]{1,0:T(8,128)S(1)} %get-tuple-element.153.own_down, ...), custom_call_target="tpu_custom_call" | custom-call | flops 3221225472 | bytes 12582912 | tf_op jit(solution)/shard_map/cond/branch_1_fun/second/pallas_call | solution.py:528
  61.7 0.1 collective-permute-start.12
  61.8 7.2 %collective-permute-start.13 = (f32[192,128]{1,0:T(8,128)S(1)}, f32[192,128]{1,0:T(8,128)S(1)}, u32[]{:S(2)}, u32[]{:S(2)}) collective-permute-start(f32[192,128]{1,0:T(8,128)S(1)} %get-tuple-element.164), channel_id=1, source_target_pairs={{1,0},{2,1},{3,2},{4,3},{5,4},{6,5},{7,6},{8,7},{9,8},{10,9},{11,1... | collective-permute-start | bytes 294920 | tf_op jit(solution)/shard_map/cond/branch_1_fun/ppermute | solution.py:467
  69.0 2.2 %restore.3 = f32[1024,256]{1,0:T(8,128)} custom-call(f32[1024,256]{1,0:T(8,128)S(1)} %get-tuple-element.160.spectra, bf16[1024,1024]{1,0:T(8,128)(2,1)S(1)} %get-tuple-element.161.back), custom_call_target="tpu_custom_call" | custom-call | flops 1073741824 | bytes 4194304 | tf_op jit(solution)/shard_map/cond/branch_1_fun/restore/pallas_call | solution.py:536
  71.2 0.6 collective-permute-done.12.from_below
  71.8 0.7 %ocean.3 = f32[2,64,128]{2,1,0:T(8,128)} custom-call(f32[2,64,128]{2,1,0:T(8,128)S(1)} %get-tuple-element.162.state, f32[192,128]{1,0:T(8,128)S(1)} %collective-permute-done.12.from_below, f32[192,128]{1,0:T(8,128)S(1)} %collective-permute-done.13.from_above, f32[128,128]{1,0:T(8,128)S(1)} %get-tuple-element.165.own_part, ...), custom_call_target="tpu_custom_call" | custom-call | flops 1048576 | bytes 262144 | tf_op jit(solution)/shard_map/cond/branch_1_fun/ocean/pallas_call | solution.py:540
  (37 shorter events, 0.1 us)
Async XLA Ops:
  0.6 17.1 %copy-start = (bf16[128,1024]{1,0:T(8,128)(2,1)S(1)}, bf16[128,1024]{1,0:T(8,128)(2,1)}, u32[]{:S(2)}) copy-start(bf16[128,1024]{1,0:T(8,128)(2,1)} %stokes_table.1) | copy-start | bytes 786436
  0.6 17.1 %copy-start.1 = (s32[4,1024,2]{1,2,0:T(2,128)S(1)}, s32[4,1024,2]{1,2,0:T(2,128)}, u32[]{:S(2)}) copy-start(s32[4,1024,2]{1,2,0:T(2,128)} %param.22) | copy-start | bytes 98308
  0.7 17.1 %copy-start.2 = (f32[4,1024,2]{1,2,0:T(2,128)S(1)}, f32[4,1024,2]{1,2,0:T(2,128)}, u32[]{:S(2)}) copy-start(f32[4,1024,2]{1,2,0:T(2,128)} %param.23) | copy-start | bytes 98308
  0.7 17.1 %copy-start.3 = (f32[2,1024]{1,0:T(2,128)S(1)}, f32[2,1024]{1,0:T(2,128)}, u32[]{:S(2)}) copy-start(f32[2,1024]{1,0:T(2,128)} %courant.1) | copy-start | bytes 24580
  0.7 17.1 %copy-start.4 = (f32[1024]{0:T(1024)S(1)}, f32[1024]{0:T(1024)}, u32[]{:S(2)}) copy-start(f32[1024]{0:T(1024)} %param.24) | copy-start | bytes 12292
  0.7 17.1 %copy-start.5 = (s32[4,256]{1,0:T(4,128)S(1)}, s32[4,256]{1,0:T(4,128)}, u32[]{:S(2)}) copy-start(s32[4,256]{1,0:T(4,128)} %point_index.1) | copy-start | bytes 12292
  0.7 17.1 %copy-start.6 = (f32[4,256]{1,0:T(4,128)S(1)}, f32[4,256]{1,0:T(4,128)}, u32[]{:S(2)}) copy-start(f32[4,256]{1,0:T(4,128)} %point_weight.1) | copy-start | bytes 12292
  0.7 17.1 %copy-start.7 = (f32[64]{0:T(128)S(1)}, f32[64]{0:T(128)}, u32[]{:S(2)}) copy-start(f32[64]{0:T(128)} %param.32) | copy-start | bytes 772
  0.7 17.1 %copy-start.12 = (s32[2,1024]{1,0:T(2,128)S(1)}, s32[2,1024]{1,0:T(2,128)}, u32[]{:S(2)}) copy-start(s32[2,1024]{1,0:T(2,128)} %sign.3) | copy-start | bytes 24580
  0.7 17.1 %copy-start.13 = (s32[4,128]{1,0:T(4,128)S(1)}, s32[4,128]{1,0:T(4,128)}, u32[]{:S(2)}) copy-start(s32[4,128]{1,0:T(4,128)} %ocean_index.3) | copy-start | bytes 6148
  0.7 17.1 %copy-start.14 = (f32[4,128]{1,0:T(4,128)S(1)}, f32[4,128]{1,0:T(4,128)}, u32[]{:S(2)}) copy-start(f32[4,128]{1,0:T(4,128)} %ocean_weight.3) | copy-start | bytes 6148
  0.7 17.1 %copy-start.15 = (f32[64]{0:T(128)S(1)}, f32[64]{0:T(128)}, u32[]{:S(2)}) copy-start(f32[64]{0:T(128)} %param.33) | copy-start | bytes 772
  3.6 28.2 %collective-permute-start.16 = (f32[632,256]{1,0:T(8,128)S(1)}, f32[632,256]{1,0:T(8,128)S(1)}, u32[]{:S(2)}, u32[]{:S(2)}) collective-permute-start(f32[632,256]{1,0:T(8,128)S(1)} %get-tuple-element.200.own_up), channel_id=1, source_target_pairs={{0,1},{1,2},{2,3},{3,4},{4,5},{5,6},{6,7},{7,8},{8,9},{9,10},{10,1... | collective-permute-start | bytes 1941512 | tf_op jit(solution)/shard_map/ppermute | solution.py:466
  6.1 25.6 %collective-permute-start.17 = (f32[632,256]{1,0:T(8,128)S(1)}, f32[632,256]{1,0:T(8,128)S(1)}, u32[]{:S(2)}, u32[]{:S(2)}) collective-permute-start(f32[632,256]{1,0:T(8,128)S(1)} %get-tuple-element.201.own_down), channel_id=1, source_target_pairs={{1,0},{2,1},{3,2},{4,3},{5,4},{6,5},{7,6},{8,7},{9,8},{10,9},{11,1... | collective-permute-start | bytes 1941512 | tf_op jit(solution)/shard_map/ppermute | solution.py:467
  15.3 15.8 %collective-permute-start.15 = (f32[64,128]{1,0:T(8,128)S(1)}, f32[64,128]{1,0:T(8,128)S(1)}, u32[]{:S(2)}, u32[]{:S(2)}) collective-permute-start(f32[64,128]{1,0:T(8,128)S(1)} %get-tuple-element.188), channel_id=1, source_target_pairs={{2,0},{3,1},{4,2},{5,3},{6,4},{7,5},{8,6},{9,7},{10,8},{11,9},{12,... | collective-permute-start | bytes 98312 | tf_op jit(solution)/shard_map/ppermute | solution.py:467
  17.7 14.0 %collective-permute-start.14 = (f32[64,128]{1,0:T(8,128)S(1)}, f32[64,128]{1,0:T(8,128)S(1)}, u32[]{:S(2)}, u32[]{:S(2)}) collective-permute-start(f32[64,128]{1,0:T(8,128)S(1)} %get-tuple-element.188), channel_id=1, source_target_pairs={{0,2},{1,3},{2,4},{3,5},{4,6},{5,7},{6,8},{7,9},{8,10},{9,11},{10,... | collective-permute-start | bytes 98312 | tf_op jit(solution)/shard_map/ppermute | solution.py:466
  25.4 6.4 %copy-start.8 = (f32[2,64,128]{2,1,0:T(8,128)S(1)}, f32[2,64,128]{2,1,0:T(8,128)}, u32[]{:S(2)}) copy-start(f32[2,64,128]{2,1,0:T(8,128)} %currents.1) | copy-start | bytes 196612
  25.4 6.4 %copy-start.9 = (f32[128]{0:T(128)S(1)}, f32[128]{0:T(128)}, u32[]{:S(2)}) copy-start(f32[128]{0:T(128)} %param.31) | copy-start | bytes 1540
  35.4 23.0 %collective-permute-start.8 = (f32[632,256]{1,0:T(8,128)S(1)}, f32[632,256]{1,0:T(8,128)S(1)}, u32[]{:S(2)}, u32[]{:S(2)}) collective-permute-start(f32[632,256]{1,0:T(8,128)S(1)} %get-tuple-element.152.own_up), channel_id=1, source_target_pairs={{0,1},{1,2},{2,3},{3,4},{4,5},{5,6},{6,7},{7,8},{8,9},{9,10},{10,1... | collective-permute-start | bytes 1941512 | tf_op jit(solution)/shard_map/cond/branch_1_fun/ppermute | solution.py:466
  35.5 22.9 %collective-permute-start.9 = (f32[632,256]{1,0:T(8,128)S(1)}, f32[632,256]{1,0:T(8,128)S(1)}, u32[]{:S(2)}, u32[]{:S(2)}) collective-permute-start(f32[632,256]{1,0:T(8,128)S(1)} %get-tuple-element.153.own_down), channel_id=1, source_target_pairs={{1,0},{2,1},{3,2},{4,3},{5,4},{6,5},{7,6},{8,7},{9,8},{10,9},{11,1... | collective-permute-start | bytes 1941512 | tf_op jit(solution)/shard_map/cond/branch_1_fun/ppermute | solution.py:467
  42.6 15.7 %collective-permute-start.10 = (f32[8,256]{1,0:T(8,128)S(1)}, f32[8,256]{1,0:T(8,128)S(1)}, u32[]{:S(2)}, u32[]{:S(2)}) collective-permute-start(f32[8,256]{1,0:T(8,128)S(1)} %get-tuple-element.154), channel_id=1, source_target_pairs={{0,2},{1,3},{2,4},{3,5},{4,6},{5,7},{6,8},{7,9},{8,10},{9,11},{10,... | collective-permute-start | bytes 24584 | tf_op jit(solution)/shard_map/cond/branch_1_fun/ppermute | solution.py:466
  42.6 15.7 %collective-permute-start.11 = (f32[8,256]{1,0:T(8,128)S(1)}, f32[8,256]{1,0:T(8,128)S(1)}, u32[]{:S(2)}, u32[]{:S(2)}) collective-permute-start(f32[8,256]{1,0:T(8,128)S(1)} %get-tuple-element.155), channel_id=1, source_target_pairs={{2,0},{3,1},{4,2},{5,3},{6,4},{7,5},{8,6},{9,7},{10,8},{11,9},{12,... | collective-permute-start | bytes 24584 | tf_op jit(solution)/shard_map/cond/branch_1_fun/ppermute | solution.py:467
  61.7 10.1 %collective-permute-start.12 = (f32[192,128]{1,0:T(8,128)S(1)}, f32[192,128]{1,0:T(8,128)S(1)}, u32[]{:S(2)}, u32[]{:S(2)}) collective-permute-start(f32[192,128]{1,0:T(8,128)S(1)} %get-tuple-element.163), channel_id=1, source_target_pairs={{0,1},{1,2},{2,3},{3,4},{4,5},{5,6},{6,7},{7,8},{8,9},{9,10},{10,1... | collective-permute-start | bytes 294920 | tf_op jit(solution)/shard_map/cond/branch_1_fun/ppermute | solution.py:466
  61.8 10.0 %collective-permute-start.13 = (f32[192,128]{1,0:T(8,128)S(1)}, f32[192,128]{1,0:T(8,128)S(1)}, u32[]{:S(2)}, u32[]{:S(2)}) collective-permute-start(f32[192,128]{1,0:T(8,128)S(1)} %get-tuple-element.164), channel_id=1, source_target_pairs={{1,0},{2,1},{3,2},{4,3},{5,4},{6,5},{7,6},{8,7},{9,8},{10,9},{11,1... | collective-permute-start | bytes 294920 | tf_op jit(solution)/shard_map/cond/branch_1_fun/ppermute | solution.py:467
  (2 other events, 12.7 us)
